TPU v7x, 256 devices: a whole 4x4x8 slice. The times are simulated.
256 devices in a mesh: region: 2 (over core), level: 128 (over z, y, x).
Axes of the slice: x: 4, y: 4, z: 8, core: 2. Of those that a mesh axis runs over, the one named last changes fastest.
Arguments:
- fine_nodes: bfloat16 [327680, 128], P(('region', 'level')), may hold values from -6 to 6
- coarse_nodes: bfloat16 [81920, 128], P(('region', 'level')), may hold values from -6 to 6
- edge_latents: bfloat16 [2097152, 128], P(('region', 'level')), may hold values from -6 to 6
- senders: int32 [2097152], P(('region', 'level')), may hold values from 0 to 1791
- receivers: int32 [2097152], P(('region', 'level')), may hold values from 0 to 1279
- live_blocks: int32 [256], P(('region', 'level')), may hold values from 1 to 64, as said below
- send_list: int32 [131072], P(('region', 'level')), may hold values from 0 to 1279
- parents: int32 [327680], P(('region', 'level')), may hold values from 0 to 40959, as said below
- edge_weight: bfloat16 [384, 128], replicated, may hold values from -0.3125 to 0.3125
- node_weights: bfloat16 [4, 256, 128], replicated, may hold values from -0.375 to 0.375
- out_weights: bfloat16 [5, 128, 128], replicated, may hold values from -0.5 to 0.5
- gains: float32 [5, 128], replicated, may hold values from 0.1 to 1.9
Outputs:
- fine_out: bfloat16 [327680, 128], P(('region', 'level'))
- coarse_out: bfloat16 [81920, 128], P(('region', 'level'))
Inputs may be any that keep to these rules, and one draw needn't show every extreme that they name: `senders`: entries below 1280 are the device's own fine nodes; the next 128 come from level index l - 1, the 128 after from level index l + 1, then 128 from each region index in order. `receivers`: own fine nodes of the device. `send_list`: each device's entries hold 128 own local node rows for the device at level index l - 1, then 128 for level index l + 1, then 128 for each region index at the same level index. `parents`: local index into the 40960 coarse nodes of the fine node's region, ordered by level index. A fine node of level index l has its parent in block l (rows l * 320 .. (l + 1) * 320 - 1), in the last 64 rows of block l - 1, or in the first 64 rows of block l + 1; every device with a lower neighbour has a fine node whose parent is row 256 of block l - 1, and every device with an upper neighbour one whose parent is row 63 of block l + 1. The first 128 * live_blocks edge slots of a device are live, the rest padding; in every draw some device has all 64 blocks live.
All inputs are finite; a program needn't handle non-finite values.
Results may differ from a plain program's by a relative error of at most 0.0063.
Values may be sent and summed in bfloat16 or wider, within the bound.
A program may use at most 64 MiB of HBM per device.

v0:
```python
import jax
import jax.numpy as jnp
from jax import lax
from jax.sharding import PartitionSpec as P

BORDER = 64


norm_eps = 1e-05
group_edges = 1024


def extended_2(x, sides, width):
    for axis, dim in sides:
        peers, length = (lax.axis_size(axis), x.shape[dim])
        up = [(i, (i + 1) % peers) for i in range(peers - 1)]
        down = [(j, i) for i, j in up]
        last = lax.slice_in_dim(x, length - width, length, axis=dim)
        initial = lax.slice_in_dim(x, 0, width, axis=dim)
        before = lax.ppermute(last, axis, up)
        after = lax.ppermute(initial, axis, down)
        x = jnp.concatenate([before, x, after], axis=dim)
    return x


def layer_norm(values, gain_row):
    centered = values - jnp.mean(values, axis=-1, keepdims=True)
    spread = jnp.mean(centered * centered, axis=-1, keepdims=True)
    return centered * lax.rsqrt(spread + norm_eps) * gain_row


def perceptron(members, weight_in, weight_out, gain_row):
    lat_width = members[0].shape[1]
    hidden = jnp.zeros((members[0].shape[0], weight_in.shape[1]), jnp.float32)
    for number, member in enumerate(members):
        hidden = hidden + jnp.dot(
            member,
            weight_in[number * lat_width : (number + 1) * lat_width],
            preferred_element_type=jnp.float32,
        )
    active = jax.nn.silu(hidden).astype(jnp.bfloat16)
    return layer_norm(jnp.dot(active, weight_out, preferred_element_type=jnp.float32), gain_row)


def residual_update(base_nodes, other_nodes, weight_in, weight_out, gain_row):
    return (
        base_nodes.astype(jnp.float32)
        + perceptron((base_nodes, other_nodes), weight_in, weight_out, gain_row)
    ).astype(jnp.bfloat16)


def coarse_section(
    fine_mid,
    coarse_nodes,
    parents,
    reach,
    nearby,
    return_sums,
    spread_new,
    node_weights,
    out_weights,
    gains,
):
    block_rows = coarse_nodes.shape[0]
    local_parent = parents - lax.axis_index("level") * block_rows + reach
    upward = perceptron((fine_mid, nearby[local_parent]), node_weights[1], out_weights[2], gains[2])
    parent_table = (
        local_parent[:, None] == jnp.arange(block_rows + 2 * reach, dtype=jnp.int32)[None, :]
    ).astype(jnp.float32)
    sums = lax.dot_general(
        parent_table,
        upward,
        (((0,), (0,)), ((), ())),
        precision=lax.Precision.HIGHEST,
        preferred_element_type=jnp.float32,
    )
    outgoing = jnp.concatenate([sums[:reach], sums[block_rows + reach :]], 0)
    returned = return_sums(outgoing)
    owned = sums[reach : reach + block_rows]
    owned = owned.at[:reach].add(returned[:reach])
    owned = owned.at[block_rows - reach :].add(returned[3 * reach :])
    coarse_out = residual_update(
        coarse_nodes, owned.astype(jnp.bfloat16), node_weights[2], out_weights[3], gains[3]
    )
    nearby_new = spread_new(coarse_out)
    fine_out = residual_update(
        fine_mid, nearby_new[local_parent], node_weights[3], out_weights[4], gains[4]
    )
    return (fine_out, coarse_out)


def body(
    fine_nodes,
    coarse_nodes,
    edge_latents,
    senders,
    receivers,
    live_blocks,
    send_list,
    parents,
    edge_weight,
    node_weights,
    out_weights,
    gains,
):
    node_count = fine_nodes.shape[0]
    slot_rows = send_list.shape[0] // (2 + lax.axis_size("region"))
    outgoing = fine_nodes[send_list]
    bordered = extended_2(outgoing[: 2 * slot_rows], (("level", 0),), slot_rows)
    received = lax.all_to_all(
        outgoing[2 * slot_rows :], "region", split_axis=0, concat_axis=0, tiled=True
    )
    extended = jnp.concatenate(
        [fine_nodes, bordered[:slot_rows], bordered[3 * slot_rows :], received], 0
    )
    live_edges = live_blocks[0] * 128
    node_ids = jnp.arange(node_count, dtype=jnp.int32)

    def add_group(group_index, running):
        edge_start = group_index * group_edges
        latents = lax.dynamic_slice_in_dim(edge_latents, edge_start, group_edges, 0)
        sender_ids = lax.dynamic_slice_in_dim(senders, edge_start, group_edges, 0)
        receiver_ids = lax.dynamic_slice_in_dim(receivers, edge_start, group_edges, 0)
        table = (receiver_ids[:, None] == node_ids[None, :]).astype(jnp.bfloat16)
        sources = extended[sender_ids]
        targets = jnp.dot(table, fine_nodes, preferred_element_type=jnp.float32).astype(
            jnp.bfloat16
        )
        message = perceptron((latents, sources, targets), edge_weight, out_weights[0], gains[0])
        updated = (latents.astype(jnp.float32) + message).astype(jnp.bfloat16)
        position = edge_start + jnp.arange(group_edges, dtype=jnp.int32)
        live_table = jnp.where((position < live_edges)[:, None], table, jnp.zeros_like(table))
        return running + lax.dot_general(
            live_table, updated, (((0,), (0,)), ((), ())), preferred_element_type=jnp.float32
        )

    group_count = (live_blocks[0] + 7) // 8
    summed = lax.fori_loop(
        0, group_count, add_group, jnp.zeros((node_count, fine_nodes.shape[1]), jnp.float32)
    )
    fine_mid = residual_update(
        fine_nodes, summed.astype(jnp.bfloat16), node_weights[0], out_weights[1], gains[1]
    )
    reach = BORDER
    nearby = extended_2(coarse_nodes, (("level", 0),), BORDER)

    def return_sums(partial_sums):
        return extended_2(partial_sums.astype(jnp.bfloat16), (("level", 0),), BORDER).astype(
            partial_sums.dtype
        )

    def spread_new(updated):
        return extended_2(updated, (("level", 0),), BORDER)

    return coarse_section(
        fine_mid,
        coarse_nodes,
        parents,
        reach,
        nearby,
        return_sums,
        spread_new,
        node_weights,
        out_weights,
        gains,
    )


def solution(mesh):
    in_specs = (
        P(("region", "level"), None),
        P(("region", "level"), None),
        P(("region", "level"), None),
        P(("region", "level")),
        P(("region", "level")),
        P(("region", "level")),
        P(("region", "level")),
        P(("region", "level")),
        P(),
        P(),
        P(),
        P(),
    )
    out_specs = (P(("region", "level"), None), P(("region", "level"), None))
    return jax.shard_map(body, mesh=mesh, in_specs=in_specs, out_specs=out_specs, check_vma=False)
```

profile of v0, /device:TPU:126, one launch (start us, length us, event | category | flops | bytes accessed | tf_op | source)
XLA Modules:
  0.0 155.8 jit_solution(4825207293967618108)
XLA Ops:
  1.4 2.1 %gather_fusion.1 = bf16[512,128]{1,0:T(8,128)(2,1)S(1)} fusion(bf16[1280,128]{1,0:T(8,128)(2,1)} %param.18, s32[1024]{0:T(1024)S(1)} %pad_clamp_fusion.1), kind=kCustom, calls=%fused_computation.1 | custom fusion | bytes 264192 | tf_op jit(solution)/shard_map/gather | solution.py:108
  3.5 4.6 %collective-permute-start = (bf16[128,128]{1,0:T(8,128)(2,1)S(1)}, bf16[128,128]{1,0:T(8,128)(2,1)S(1)}, u32[]{:S(2)}, u32[]{:S(2)}) collective-permute-start(bf16[128,128]{1,0:T(8,128)(2,1)S(1)} %get-tuple-element.162), channel_id=1, source_target_pairs={{0,1},{1,2},{2,3},{3,4},{4,5},{5,6},{6,7},{7,8},{8,9},{9,10},{10,1... | collective-permute-start | bytes 98312 | tf_op jit(solution)/shard_map/ppermute | solution.py:20
  8.1 1.9 %collective-permute-start.1 = (bf16[128,128]{1,0:T(8,128)(2,1)S(1)}, bf16[128,128]{1,0:T(8,128)(2,1)S(1)}, u32[]{:S(2)}, u32[]{:S(2)}) collective-permute-start(bf16[128,128]{1,0:T(8,128)(2,1)S(1)} %get-tuple-element.163), channel_id=1, source_target_pairs={{1,0},{2,1},{3,2},{4,3},{5,4},{6,5},{7,6},{8,7},{9,8},{10,9},{11,1... | collective-permute-start | bytes 98312 | tf_op jit(solution)/shard_map/ppermute | solution.py:21
  10.7 3.3 %all-to-all-start = ((bf16[2,128,128]{2,1,0:T(8,128)(2,1)}), bf16[2,128,128]{2,1,0:T(8,128)(2,1)S(1)}, u32[]{:S(2)}, u32[]{:S(2)}) async-start(bf16[2,128,128]{2,1,0:T(8,128)(2,1)} %bitcast.3), calls=%async_computation | async-start | bytes 131072 | tf_op jit(solution)/shard_map/all_to_all | solution.py:110
  14.7 9.3 %collective-permute-start.2 = (bf16[64,128]{1,0:T(8,128)(2,1)S(1)}, bf16[64,128]{1,0:T(8,128)(2,1)S(1)}, u32[]{:S(2)}, u32[]{:S(2)}) collective-permute-start(bf16[64,128]{1,0:T(8,128)(2,1)S(1)} %get-tuple-element.168), channel_id=1, source_target_pairs={{0,1},{1,2},{2,3},{3,4},{4,5},{5,6},{6,7},{7,8},{8,9},{9,10},{10,1... | collective-permute-start | bytes 49160 | tf_op jit(solution)/shard_map/ppermute | solution.py:20
  24.1 1.9 %collective-permute-start.3 = (bf16[64,128]{1,0:T(8,128)(2,1)S(1)}, bf16[64,128]{1,0:T(8,128)(2,1)S(1)}, u32[]{:S(2)}, u32[]{:S(2)}) collective-permute-start(bf16[64,128]{1,0:T(8,128)(2,1)S(1)} %get-tuple-element.169), channel_id=1, source_target_pairs={{1,0},{2,1},{3,2},{4,3},{5,4},{6,5},{7,6},{8,7},{9,8},{10,9},{11,1... | collective-permute-start | bytes 49160 | tf_op jit(solution)/shard_map/ppermute | solution.py:21
  26.0 2.0 %fusion.69 = f32[1280,128]{1,0:T(8,128)} fusion(bf16[1280,128]{1,0:T(8,128)(2,1)} %param.18, bf16[4,256,128]{2,1,0:T(8,128)(2,1)} %param.27), kind=kOutput, calls=%fused_computation.95 | convolution fusion | flops 41943040 | bytes 1015808 | tf_op jit(solution)/shard_map/dot_general | solution.py:36
  29.5 5.6 %collective-permute-done.3 = bf16[64,128]{1,0:T(8,128)(2,1)S(1)} collective-permute-done((bf16[64,128]{1,0:T(8,128)(2,1)S(1)}, bf16[64,128]{1,0:T(8,128)(2,1)S(1)}, u32[]{:S(2)}, u32[]{:S(2)}) %collective-permute-start.3) | collective-permute-done | bytes 16416 | tf_op jit(solution)/shard_map/ppermute | solution.py:21
  35.2 3.5 %gather_fusion.2 = bf16[1280,128]{1,0:T(8,128)(2,1)} fusion(bf16[448,128]{1,0:T(8,128)(2,1)S(1)} %pad_maximum_fusion.1, s32[2048]{0:T(1024)S(1)} %pad_clamp_fusion), kind=kCustom, calls=%fused_computation.2 | custom fusion | bytes 660480 | tf_op jit(solution)/shard_map/gather | solution.py:66
  38.8 80.5 %while.13 = (s32[]{:T(128)}, f32[1280,128]{1,0:T(8,128)S(1)}, s32[]{:T(128)}, s32[]{:T(128)}, s32[8192]{0:T(1024)}, /*index=5*/bf16[8192,128]{1,0:T(8,128)(2,1)}...) while((s32[]{:T(128)}, f32[1280,128]{1,0:T(8,128)S(1)}, ...), condition=%wide.region_3.4_spmd.clone, body=%wide.region_0.3_spmd.clone.sunk | while | flops 813079552 | bytes 8392407 | solution.py:138
  40.7 3.2 %gather_fusion = bf16[1024,128]{1,0:T(8,128)(2,1)S(1)} fusion(bf16[1792,128]{1,0:T(8,128)(2,1)S(1)} %get-tuple-element.304, s32[1024]{0:T(1024)S(1)} %fusion.144), kind=kCustom, calls=%fused_computation.clone.clone.1 | custom fusion | bytes 528384 | tf_op jit(solution)/shard_map/while/body/gather | solution.py:125
  47.4 1.5 fusion.146
  50.8 3.2 %gather_fusion = bf16[1024,128]{1,0:T(8,128)(2,1)S(1)} fusion(bf16[1792,128]{1,0:T(8,128)(2,1)S(1)} %get-tuple-element.304, s32[1024]{0:T(1024)S(1)} %fusion.144), kind=kCustom, calls=%fused_computation.clone.clone.1 | custom fusion | bytes 528384 | tf_op jit(solution)/shard_map/while/body/gather | solution.py:125
  60.9 3.2 %gather_fusion = bf16[1024,128]{1,0:T(8,128)(2,1)S(1)} fusion(bf16[1792,128]{1,0:T(8,128)(2,1)S(1)} %get-tuple-element.304, s32[1024]{0:T(1024)S(1)} %fusion.144), kind=kCustom, calls=%fused_computation.clone.clone.1 | custom fusion | bytes 528384 | tf_op jit(solution)/shard_map/while/body/gather | solution.py:125
  67.5 1.5 fusion.146
  70.9 3.2 %gather_fusion = bf16[1024,128]{1,0:T(8,128)(2,1)S(1)} fusion(bf16[1792,128]{1,0:T(8,128)(2,1)S(1)} %get-tuple-element.304, s32[1024]{0:T(1024)S(1)} %fusion.144), kind=kCustom, calls=%fused_computation.clone.clone.1 | custom fusion | bytes 528384 | tf_op jit(solution)/shard_map/while/body/gather | solution.py:125
  77.6 1.5 fusion.146
  81.0 3.2 %gather_fusion = bf16[1024,128]{1,0:T(8,128)(2,1)S(1)} fusion(bf16[1792,128]{1,0:T(8,128)(2,1)S(1)} %get-tuple-element.304, s32[1024]{0:T(1024)S(1)} %fusion.144), kind=kCustom, calls=%fused_computation.clone.clone.1 | custom fusion | bytes 528384 | tf_op jit(solution)/shard_map/while/body/gather | solution.py:125
  87.6 1.5 fusion.146
  91.0 3.2 %gather_fusion = bf16[1024,128]{1,0:T(8,128)(2,1)S(1)} fusion(bf16[1792,128]{1,0:T(8,128)(2,1)S(1)} %get-tuple-element.304, s32[1024]{0:T(1024)S(1)} %fusion.144), kind=kCustom, calls=%fused_computation.clone.clone.1 | custom fusion | bytes 528384 | tf_op jit(solution)/shard_map/while/body/gather | solution.py:125
  97.7 1.5 fusion.146
  101.1 3.2 %gather_fusion = bf16[1024,128]{1,0:T(8,128)(2,1)S(1)} fusion(bf16[1792,128]{1,0:T(8,128)(2,1)S(1)} %get-tuple-element.304, s32[1024]{0:T(1024)S(1)} %fusion.144), kind=kCustom, calls=%fused_computation.clone.clone.1 | custom fusion | bytes 528384 | tf_op jit(solution)/shard_map/while/body/gather | solution.py:125
  111.2 3.2 %gather_fusion = bf16[1024,128]{1,0:T(8,128)(2,1)S(1)} fusion(bf16[1792,128]{1,0:T(8,128)(2,1)S(1)} %get-tuple-element.304, s32[1024]{0:T(1024)S(1)} %fusion.144), kind=kCustom, calls=%fused_computation.clone.clone.1 | custom fusion | bytes 528384 | tf_op jit(solution)/shard_map/while/body/gather | solution.py:125
  119.3 1.6 %fusion.96 = (f32[1280]{0:T(1024)S(1)}, f32[1280,128]{0,1:T(8,128)S(1)}) fusion(bf16[5,128,128]{2,1,0:T(8,128)(2,1)} %get-tuple-element.313, f32[1280,128]{1,0:T(8,128)} %fusion.69, f32[1280,128]{1,0:T(8,128)S(1)} %get-tuple-element.94, bf16[4,256,128]{2,1,0:T(8,128)(2,1)} %param.27), kind=kOutput, calls=%fused_computation.138 | convolution fusion | flops 85195520 | bytes 2036736 | tf_op jit(solution)/shard_map/dot_general | solution.py:42
  122.6 1.8 %fusion.104 = (bf16[448,128]{1,0:T(8,128)(2,1)S(1)}, f32[448,128]{1,0:T(8,128)S(1)}) fusion(f32[1280,128]{0,1:T(8,128)S(1)} %get-tuple-element.179, f32[128]{0:T(128)S(1)} %copy-done.9, f32[1280]{0:T(1024)S(1)} %add_rsqrt_fusion.2, f32[1280]{0:T(1024)S(1)} %broadcast_multiply_fusion.2, s32[1280]{0:T(1024)S(1)} %get-tuple-element.171), kind=kOutput, calls=%fused_computation.140 | convolution fusion | flops 882499584 | bytes 1015296 | tf_op jit(solution)/shard_map/dot_general | solution.py:70
  124.4 1.9 %collective-permute-start.4 = (bf16[64,128]{1,0:T(8,128)(2,1)S(1)}, bf16[64,128]{1,0:T(8,128)(2,1)S(1)}, u32[]{:S(2)}, u32[]{:S(2)}) collective-permute-start(bf16[64,128]{1,0:T(8,128)(2,1)S(1)} %get-tuple-element.164), channel_id=1, source_target_pairs={{0,1},{1,2},{2,3},{3,4},{4,5},{5,6},{6,7},{7,8},{8,9},{9,10},{10,1... | collective-permute-start | bytes 49160 | tf_op jit(solution)/shard_map/ppermute | solution.py:20
  126.4 3.9 %collective-permute-start.5 = (bf16[64,128]{1,0:T(8,128)(2,1)S(1)}, bf16[64,128]{1,0:T(8,128)(2,1)S(1)}, u32[]{:S(2)}, u32[]{:S(2)}) collective-permute-start(bf16[64,128]{1,0:T(8,128)(2,1)S(1)} %get-tuple-element.165), channel_id=1, source_target_pairs={{1,0},{2,1},{3,2},{4,3},{5,4},{6,5},{7,6},{8,7},{9,8},{10,9},{11,1... | collective-permute-start | bytes 49160 | tf_op jit(solution)/shard_map/ppermute | solution.py:21
  130.5 6.9 %collective-permute-done.5 = bf16[64,128]{1,0:T(8,128)(2,1)S(1)} collective-permute-done((bf16[64,128]{1,0:T(8,128)(2,1)S(1)}, bf16[64,128]{1,0:T(8,128)(2,1)S(1)}, u32[]{:S(2)}, u32[]{:S(2)}) %collective-permute-start.5) | collective-permute-done | bytes 16416 | tf_op jit(solution)/shard_map/ppermute | solution.py:21
  138.3 1.9 %collective-permute-start.6 = (bf16[64,128]{1,0:T(8,128)(2,1)S(1)}, bf16[64,128]{1,0:T(8,128)(2,1)S(1)}, u32[]{:S(2)}, u32[]{:S(2)}) collective-permute-start(bf16[64,128]{1,0:T(8,128)(2,1)S(1)} %get-tuple-element.166), channel_id=1, source_target_pairs={{0,1},{1,2},{2,3},{3,4},{4,5},{5,6},{6,7},{7,8},{8,9},{9,10},{10,1... | collective-permute-start | bytes 49160 | tf_op jit(solution)/shard_map/ppermute | solution.py:20
  140.2 3.9 %collective-permute-start.7 = (bf16[64,128]{1,0:T(8,128)(2,1)S(1)}, bf16[64,128]{1,0:T(8,128)(2,1)S(1)}, u32[]{:S(2)}, u32[]{:S(2)}) collective-permute-start(bf16[64,128]{1,0:T(8,128)(2,1)S(1)} %get-tuple-element.167), channel_id=1, source_target_pairs={{1,0},{2,1},{3,2},{4,3},{5,4},{6,5},{7,6},{8,7},{9,8},{10,9},{11,1... | collective-permute-start | bytes 49160 | tf_op jit(solution)/shard_map/ppermute | solution.py:21
  144.4 6.8 %collective-permute-done.7 = bf16[64,128]{1,0:T(8,128)(2,1)S(1)} collective-permute-done((bf16[64,128]{1,0:T(8,128)(2,1)S(1)}, bf16[64,128]{1,0:T(8,128)(2,1)S(1)}, u32[]{:S(2)}, u32[]{:S(2)}) %collective-permute-start.7) | collective-permute-done | bytes 16416 | tf_op jit(solution)/shard_map/ppermute | solution.py:21
  151.3 2.8 %gather_fusion.3 = bf16[1280,128]{1,0:T(8,128)(2,1)S(1)} fusion(bf16[448,128]{1,0:T(8,128)(2,1)S(1)} %pad_maximum_fusion.2, s32[2048]{0:T(1024)S(1)} %pad_clamp_fusion), kind=kCustom, calls=%fused_computation.3 | custom fusion | bytes 660480 | tf_op jit(solution)/shard_map/gather | solution.py:87
  (173 shorter events, 54.1 us)
Async XLA Ops:
  0.6 28.6 %copy-start = (bf16[1280,128]{1,0:T(8,128)(2,1)S(1)}, bf16[1280,128]{1,0:T(8,128)(2,1)}, u32[]{:S(2)}) copy-start(bf16[1280,128]{1,0:T(8,128)(2,1)} %param.18) | copy-start | bytes 983044
  0.6 34.5 %copy-start.2 = (bf16[320,128]{1,0:T(8,128)(2,1)S(1)}, bf16[320,128]{1,0:T(8,128)(2,1)}, u32[]{:S(2)}) copy-start(bf16[320,128]{1,0:T(8,128)(2,1)} %param.19) | copy-start | bytes 245764
  0.7 27.4 %copy-start.8 = (f32[5,128]{1,0:T(8,128)S(1)}, f32[5,128]{1,0:T(8,128)}, u32[]{:S(2)}) copy-start(f32[5,128]{1,0:T(8,128)} %param.29) | copy-start | bytes 7684
  0.7 27.9 %copy-start.7 = (s32[1280]{0:T(1024)S(1)}, s32[1280]{0:T(1024)}, u32[]{:S(2)}) copy-start(s32[1280]{0:T(1024)} %param.25) | copy-start | bytes 15364
  3.5 35.2 %collective-permute-start = (bf16[128,128]{1,0:T(8,128)(2,1)S(1)}, bf16[128,128]{1,0:T(8,128)(2,1)S(1)}, u32[]{:S(2)}, u32[]{:S(2)}) collective-permute-start(bf16[128,128]{1,0:T(8,128)(2,1)S(1)} %get-tuple-element.162), channel_id=1, source_target_pairs={{0,1},{1,2},{2,3},{3,4},{4,5},{5,6},{6,7},{7,8},{8,9},{9,10},{10,1... | collective-permute-start | bytes 98312 | tf_op jit(solution)/shard_map/ppermute | solution.py:20
  8.1 30.6 %collective-permute-start.1 = (bf16[128,128]{1,0:T(8,128)(2,1)S(1)}, bf16[128,128]{1,0:T(8,128)(2,1)S(1)}, u32[]{:S(2)}, u32[]{:S(2)}) collective-permute-start(bf16[128,128]{1,0:T(8,128)(2,1)S(1)} %get-tuple-element.163), channel_id=1, source_target_pairs={{1,0},{2,1},{3,2},{4,3},{5,4},{6,5},{7,6},{8,7},{9,8},{10,9},{11,1... | collective-permute-start | bytes 98312 | tf_op jit(solution)/shard_map/ppermute | solution.py:21
  10.7 28.0 %all-to-all-start = ((bf16[2,128,128]{2,1,0:T(8,128)(2,1)}), bf16[2,128,128]{2,1,0:T(8,128)(2,1)S(1)}, u32[]{:S(2)}, u32[]{:S(2)}) async-start(bf16[2,128,128]{2,1,0:T(8,128)(2,1)} %bitcast.3), calls=%async_computation | async-start | bytes 131072 | tf_op jit(solution)/shard_map/all_to_all | solution.py:110
  14.7 14.8 %collective-permute-start.2 = (bf16[64,128]{1,0:T(8,128)(2,1)S(1)}, bf16[64,128]{1,0:T(8,128)(2,1)S(1)}, u32[]{:S(2)}, u32[]{:S(2)}) collective-permute-start(bf16[64,128]{1,0:T(8,128)(2,1)S(1)} %get-tuple-element.168), channel_id=1, source_target_pairs={{0,1},{1,2},{2,3},{3,4},{4,5},{5,6},{6,7},{7,8},{8,9},{9,10},{10,1... | collective-permute-start | bytes 49160 | tf_op jit(solution)/shard_map/ppermute | solution.py:20
  24.1 11.1 %collective-permute-start.3 = (bf16[64,128]{1,0:T(8,128)(2,1)S(1)}, bf16[64,128]{1,0:T(8,128)(2,1)S(1)}, u32[]{:S(2)}, u32[]{:S(2)}) collective-permute-start(bf16[64,128]{1,0:T(8,128)(2,1)S(1)} %get-tuple-element.169), channel_id=1, source_target_pairs={{1,0},{2,1},{3,2},{4,3},{5,4},{6,5},{7,6},{8,7},{9,8},{10,9},{11,1... | collective-permute-start | bytes 49160 | tf_op jit(solution)/shard_map/ppermute | solution.py:21
  35.2 3.6 %copy-start.1 = (bf16[384,128]{1,0:T(8,128)(2,1)S(1)}, bf16[384,128]{1,0:T(8,128)(2,1)}, u32[]{:S(2)}) copy-start(bf16[384,128]{1,0:T(8,128)(2,1)} %param.26) | copy-start | bytes 294916
  119.3 1.9 %copy-start.6 = (bf16[4,256,128]{2,1,0:T(8,128)(2,1)S(1)}, bf16[4,256,128]{2,1,0:T(8,128)(2,1)}, u32[]{:S(2)}) copy-start(bf16[4,256,128]{2,1,0:T(8,128)(2,1)} %param.27) | copy-start | bytes 786436
  121.0 1.0 copy-start.4
  121.0 1.0 copy-start.5
  122.0 0.6 copy-start.9
  124.4 6.0 %collective-permute-start.4 = (bf16[64,128]{1,0:T(8,128)(2,1)S(1)}, bf16[64,128]{1,0:T(8,128)(2,1)S(1)}, u32[]{:S(2)}, u32[]{:S(2)}) collective-permute-start(bf16[64,128]{1,0:T(8,128)(2,1)S(1)} %get-tuple-element.164), channel_id=1, source_target_pairs={{0,1},{1,2},{2,3},{3,4},{4,5},{5,6},{6,7},{7,8},{8,9},{9,10},{10,1... | collective-permute-start | bytes 49160 | tf_op jit(solution)/shard_map/ppermute | solution.py:20
  126.4 11.1 %collective-permute-start.5 = (bf16[64,128]{1,0:T(8,128)(2,1)S(1)}, bf16[64,128]{1,0:T(8,128)(2,1)S(1)}, u32[]{:S(2)}, u32[]{:S(2)}) collective-permute-start(bf16[64,128]{1,0:T(8,128)(2,1)S(1)} %get-tuple-element.165), channel_id=1, source_target_pairs={{1,0},{2,1},{3,2},{4,3},{5,4},{6,5},{7,6},{8,7},{9,8},{10,9},{11,1... | collective-permute-start | bytes 49160 | tf_op jit(solution)/shard_map/ppermute | solution.py:21
  138.3 15.8 %copy-start.3 = (bf16[320,128]{1,0:T(8,128)(2,1)}, bf16[320,128]{1,0:T(8,128)(2,1)S(1)}, u32[]{:S(2)}) copy-start(bf16[320,128]{1,0:T(8,128)(2,1)S(1)} %add_convert_fusion.4) | copy-start | bytes 245764
  138.3 6.1 %collective-permute-start.6 = (bf16[64,128]{1,0:T(8,128)(2,1)S(1)}, bf16[64,128]{1,0:T(8,128)(2,1)S(1)}, u32[]{:S(2)}, u32[]{:S(2)}) collective-permute-start(bf16[64,128]{1,0:T(8,128)(2,1)S(1)} %get-tuple-element.166), channel_id=1, source_target_pairs={{0,1},{1,2},{2,3},{3,4},{4,5},{5,6},{6,7},{7,8},{8,9},{9,10},{10,1... | collective-permute-start | bytes 49160 | tf_op jit(solution)/shard_map/ppermute | solution.py:20
  140.2 11.1 %collective-permute-start.7 = (bf16[64,128]{1,0:T(8,128)(2,1)S(1)}, bf16[64,128]{1,0:T(8,128)(2,1)S(1)}, u32[]{:S(2)}, u32[]{:S(2)}) collective-permute-start(bf16[64,128]{1,0:T(8,128)(2,1)S(1)} %get-tuple-element.167), channel_id=1, source_target_pairs={{1,0},{2,1},{3,2},{4,3},{5,4},{6,5},{7,6},{8,7},{9,8},{10,9},{11,1... | collective-permute-start | bytes 49160 | tf_op jit(solution)/shard_map/ppermute | solution.py:21
where the time goes:
time: 156 us
  local copies, waits for them, and re-layouts  52.2 us (33%)
  matrix products  40.7 us (26%)
  starting transfers between devices  32.8 us (21%)
  waiting for transfers between devices  19.4 us (12%)
  other arithmetic  8.1 us (5%)
  between operations  1.74 us (1%)
    gather x8, local copies, waits for them, and re-layouts, add_group(): sources = extended[sender_ids]  25.6 us
    ppermute x4, waiting for transfers between devices, extended_2(): after = lax.ppermute(initial, axis, down)  19.4 us
    ppermute x4, starting transfers between devices, extended_2(): before = lax.ppermute(last, axis, up)  17.8 us
    dot_general x28, matrix products, perceptron(): jnp.dot(member, weight_in[number * lat_width:(number + 1) * lat_width], p...  15.7 us
    dot_general x8, matrix products, add_group(): lax.dot_general(live_table, updated, (((0,), (0,)), ((), ())), preferred_...  11.9 us
    ppermute x4, starting transfers between devices, extended_2(): after = lax.ppermute(initial, axis, down)  11.7 us
    dot_general x12, matrix products, perceptron(): jnp.dot(active, weight_out, preferred_element_type=jnp.float32)  11.3 us
    dynamic_slice x16, local copies, waits for them, and re-layouts, add_group(): latents = lax.dynamic_slice_in_dim(edge_latents, edge_start, group_edges, 0)  8.99 us
  transfers between devices with their start and end apart: 9, of which 3 were waited for; matrix products, arithmetic and copies ran while one was open for 5% of the time, Pallas kernels for 0%

commit v1 on v0

v1 whole, which is shorter than its diff:
```python
import functools

import jax
import jax.numpy as jnp
from jax import lax
from jax.experimental import pallas as pl
from jax.experimental.pallas import tpu as pltpu
from jax.sharding import PartitionSpec as P

MESH = pl.DeviceIdType.MESH
F32 = jnp.float32
BF16 = jnp.bfloat16
LAT = 128
BORDER = 64
SLOT = 128
norm_eps = 1e-05
group_edges = 1024
TILE = 256


def dot(a, b, ca=1, cb=0):
    return lax.dot_general(a, b, (((ca,), (cb,)), ((), ())), preferred_element_type=F32)


def silu(v):
    h = 0.5 * v
    return (h * jnp.tanh(h) + h).astype(BF16)


def norm_rows(o):
    c = o - jnp.mean(o, axis=1, keepdims=True)
    return c * lax.rsqrt(jnp.mean(c * c, axis=1, keepdims=True) + norm_eps)


def norm_columns(o):
    c = o - jnp.mean(o, axis=0, keepdims=True)
    return c * lax.rsqrt(jnp.mean(c * c, axis=0, keepdims=True) + norm_eps)


def one_hot_columns(low, rows):
    shape = (rows, low.shape[1])
    ids = lax.broadcasted_iota(jnp.int32, shape, 0).astype(BF16)
    return jnp.where(ids == jnp.broadcast_to(low, shape), jnp.ones((), BF16), jnp.zeros((), BF16))


def split(x):
    high = x.astype(BF16)
    return jnp.concatenate([high, (x - high.astype(F32)).astype(BF16)], axis=1)


def pick(products, high, count):
    x = products[:LAT]
    for g in range(1, count):
        x = jnp.where(high == g, products[g * LAT : (g + 1) * LAT], x)
    return x


def low_high(ids):
    return (ids & (TILE - 1)).astype(F32).astype(BF16), ids >> 8


def kernel(
    levels,
    fine,
    coarse,
    latents,
    senders,
    receivers,
    live,
    send_list,
    parents,
    edge_w,
    node_w,
    out_w,
    gains,
    fine_out,
    coarse_out,
    lat_v,
    sender_t,
    receiver_t,
    outgoing,
    arrived,
    cext,
    par_rows,
    par_cols,
    up_pre,
    down_pre,
    mid,
    sums_out,
    sums_in,
    acc,
    weights_t,
    gain_t,
    lat_sem,
    send_sem,
    recv_sem,
):
    r, l = lax.axis_index("region"), lax.axis_index("level")
    nodes, blocks = fine.shape[0], coarse.shape[0]
    ext = blocks + 2 * BORDER
    groups = nodes // TILE
    slots = arrived.shape[0]
    edges = latents.shape[0]
    has_lower, has_upper = l > 0, l < levels - 1
    lower, upper, peer = (r, l - 1), (r, l + 1), (1 - r, l)

    load = pltpu.make_async_copy(latents, lat_v, lat_sem)
    load.start()

    barrier = pltpu.get_barrier_semaphore()
    pl.semaphore_signal(barrier, inc=1, device_id=peer, device_id_type=MESH)

    @pl.when(has_lower)
    def _():
        pl.semaphore_signal(barrier, inc=1, device_id=lower, device_id_type=MESH)

    @pl.when(has_upper)
    def _():
        pl.semaphore_signal(barrier, inc=1, device_id=upper, device_id_type=MESH)

    def remote(kind, src, dst, device):
        return pltpu.make_async_remote_copy(
            src_ref=src,
            dst_ref=dst,
            send_sem=send_sem.at[kind],
            recv_sem=recv_sem.at[kind],
            device_id=device,
            device_id_type=MESH,
        )

    halo_down = remote(0, outgoing.at[0], arrived.at[1], lower)
    halo_up = remote(1, outgoing.at[1], arrived.at[0], upper)
    halo_peer = remote(2, outgoing.at[3 - r], arrived.at[2 + r], peer)
    coarse_down = remote(
        3, coarse.at[pl.ds(0, BORDER)], cext.at[pl.ds(BORDER + blocks, BORDER)], lower
    )
    coarse_up = remote(
        4, coarse.at[pl.ds(blocks - BORDER, BORDER)], cext.at[pl.ds(0, BORDER)], upper
    )
    sums_down = remote(5, sums_out.at[pl.ds(0, 2 * BORDER)], sums_in.at[1], lower)
    sums_up = remote(6, sums_out.at[pl.ds(blocks, 2 * BORDER)], sums_in.at[0], upper)

    w_sender = edge_w[LAT : 2 * LAT, :].T
    w_receiver = edge_w[2 * LAT :, :].T
    w_both = jnp.concatenate([w_sender, w_receiver], axis=0)
    for g in range(groups):
        both = dot(w_both, fine[g * TILE : (g + 1) * TILE, :], 1, 1).astype(BF16)
        sender_t[g * LAT : (g + 1) * LAT, :] = both[:LAT]
        receiver_t[g * LAT : (g + 1) * LAT, :] = both[LAT:]

    sends = jnp.concatenate([send_list[j : j + 1, :] for j in range(slots)], axis=1)
    low, high = low_high(sends)
    picked = pick(
        dot(sender_t[: groups * LAT, :], one_hot_columns(low, TILE)), high, groups
    ).astype(BF16)
    for j in range(slots):
        outgoing[j] = picked[:, j * SLOT : (j + 1) * SLOT]

    pl.semaphore_wait(barrier, 1 + has_lower.astype(jnp.int32) + has_upper.astype(jnp.int32))
    halo_peer.start()

    @pl.when(has_lower)
    def _():
        halo_down.start()
        coarse_down.start()

    @pl.when(has_upper)
    def _():
        halo_up.start()
        coarse_up.start()

    arrived[2 + r] = outgoing[2 + r]
    cext[BORDER : BORDER + blocks, :] = coarse[...]
    cext[ext:, :] = jnp.zeros((cext.shape[0] - ext, LAT), BF16)

    @pl.when(jnp.logical_not(has_lower))
    def _():
        arrived[0] = jnp.zeros((LAT, SLOT), BF16)
        cext[:BORDER, :] = jnp.zeros((BORDER, LAT), BF16)
        sums_in[0] = jnp.zeros((2 * BORDER, LAT), BF16)

    @pl.when(jnp.logical_not(has_upper))
    def _():
        arrived[1] = jnp.zeros((LAT, SLOT), BF16)
        cext[BORDER + blocks : ext, :] = jnp.zeros((BORDER, LAT), BF16)
        sums_in[1] = jnp.zeros((2 * BORDER, LAT), BF16)

    weights_t[:LAT, :] = edge_w[:LAT, :].T
    eye = lax.broadcasted_iota(jnp.int32, (LAT, LAT), 0) == lax.broadcasted_iota(
        jnp.int32, (LAT, LAT), 1
    )
    weights_t[LAT : 2 * LAT, :] = jnp.where(eye, 1.0, 0.0).astype(BF16)
    weights_t[2 * LAT :, :] = out_w[0].T
    gain_t[...] = jnp.broadcast_to(gains[0:1, :], (LAT, LAT)).T
    acc[...] = jnp.zeros_like(acc)
    offset = BORDER - l * blocks
    width = par_cols.shape[0]
    for j in range(nodes // LAT):
        place = (parents[j : j + 1, :] + offset).astype(F32)
        wide = jnp.broadcast_to(place, (width, LAT))
        ids = lax.broadcasted_iota(jnp.int32, (width, LAT), 0).astype(F32)
        par_cols[:, j * LAT : (j + 1) * LAT] = jnp.where(ids == wide, 1.0, 0.0).astype(BF16)
        column = jnp.broadcast_to(place, (LAT, LAT)).T
        ids = lax.broadcasted_iota(jnp.int32, (LAT, LAT), 1).astype(F32)
        for k in range(width // LAT):
            par_rows[j * LAT : (j + 1) * LAT, k * LAT : (k + 1) * LAT] = jnp.where(
                ids + float(k * LAT) == column, 1.0, 0.0
            ).astype(BF16)

    halo_peer.wait()

    @pl.when(has_lower)
    def _():
        halo_down.wait_send()
        halo_up.wait_recv()
        coarse_down.wait_send()
        coarse_up.wait_recv()

    @pl.when(has_upper)
    def _():
        halo_up.wait_send()
        halo_down.wait_recv()
        coarse_up.wait_send()
        coarse_down.wait_recv()

    for j in range(slots // 2):
        g = groups + j
        sender_t[g * LAT : (g + 1) * LAT, :] = jnp.concatenate(
            [arrived[2 * j], arrived[2 * j + 1]], axis=1
        )

    up_table = split(dot(cext[...], node_w[1, LAT:, :]))
    for g in range(groups):
        rows = slice(g * TILE, (g + 1) * TILE)
        found = dot(par_rows[rows, :], up_table)
        up_pre[rows, :] = found[:, :LAT] + found[:, LAT:]

    load.wait()
    sub = group_edges // LAT

    def add_group(b, carry):
        def row(ref):
            return jnp.concatenate([ref[pl.ds(b * sub + j, 1), :] for j in range(sub)], axis=1)

        s_low, s_high = low_high(row(senders))
        r_low, r_high = low_high(row(receivers))
        lat = lat_v[pl.ds(pl.multiple_of(b * group_edges, group_edges), group_edges), :]
        first = dot(weights_t[: 2 * LAT, :], lat, 1, 1)
        r_hot = one_hot_columns(r_low, TILE)
        hidden = first[:LAT] + pick(dot(sender_t[...], one_hot_columns(s_low, TILE)), s_high, 7)
        hidden = hidden + pick(dot(receiver_t[...], r_hot), r_high, groups)
        message = norm_columns(dot(weights_t[2 * LAT :, :], silu(hidden)))
        updated = (first[LAT:] + message * jnp.concatenate([gain_t[...]] * sub, axis=1)).astype(BF16)
        position = b * group_edges + lax.broadcasted_iota(jnp.int32, (1, group_edges), 1)
        target = jnp.where(position < live[0] * 128, r_high, groups)
        spread = jnp.concatenate(
            [
                updated
                * jnp.broadcast_to(jnp.where(target == g, 1.0, 0.0).astype(BF16), updated.shape)
                for g in range(groups)
            ],
            axis=0,
        )
        acc[...] += dot(spread, r_hot, 1, 1)
        return carry

    lax.fori_loop(0, edges // group_edges, add_group, 0)

    sums = jnp.zeros((width, 2 * LAT), F32)
    for g in range(groups):
        rows = slice(g * TILE, (g + 1) * TILE)
        own = fine[rows, :]
        agg = acc[g * LAT : (g + 1) * LAT, :].T.astype(BF16)
        hidden = dot(jnp.concatenate([own, agg], axis=1), node_w[0])
        new = norm_rows(dot(silu(hidden), out_w[1])) * gains[1:2, :]
        new = (own.astype(F32) + new).astype(BF16)
        mid[rows, :] = new
        hidden = dot(new, node_w[1, :LAT, :]) + up_pre[rows, :]
        upward = norm_rows(dot(silu(hidden), out_w[2])) * gains[2:3, :]
        sums = sums + dot(par_cols[:, rows], split(upward))
    sums = sums[:, :LAT] + sums[:, LAT:]
    sums_out[...] = sums[:ext].astype(BF16)

    @pl.when(has_lower)
    def _():
        sums_down.start()

    @pl.when(has_upper)
    def _():
        sums_up.start()

    for g in range(groups):
        rows = slice(g * TILE, (g + 1) * TILE)
        down_pre[rows, :] = dot(mid[rows, :], node_w[3, :LAT, :])

    @pl.when(has_lower)
    def _():
        sums_down.wait_send()
        sums_up.wait_recv()

    @pl.when(has_upper)
    def _():
        sums_up.wait_send()
        sums_down.wait_recv()

    total = jnp.concatenate(
        [
            sums[: 2 * BORDER] + sums_in[0].astype(F32),
            sums[2 * BORDER : blocks],
            sums[blocks:ext] + sums_in[1].astype(F32),
        ],
        axis=0,
    ).astype(BF16)
    base = cext[:ext, :]
    hidden = dot(jnp.concatenate([base, total], axis=1), node_w[2])
    new = norm_rows(dot(silu(hidden), out_w[3])) * gains[3:4, :]
    new = (base.astype(F32) + new).astype(BF16)
    coarse_out[...] = new[BORDER : BORDER + blocks]
    down_table = split(dot(new, node_w[3, LAT:, :]))
    for g in range(groups):
        rows = slice(g * TILE, (g + 1) * TILE)
        found = dot(par_rows[rows, :ext], down_table)
        hidden = down_pre[rows, :] + found[:, :LAT] + found[:, LAT:]
        new = norm_rows(dot(silu(hidden), out_w[4])) * gains[4:5, :]
        fine_out[rows, :] = (mid[rows, :].astype(F32) + new).astype(BF16)


def body(
    levels,
    fine_nodes,
    coarse_nodes,
    edge_latents,
    senders,
    receivers,
    live_blocks,
    send_list,
    parents,
    edge_weight,
    node_weights,
    out_weights,
    gains,
):
    nodes, blocks, edges = fine_nodes.shape[0], coarse_nodes.shape[0], edge_latents.shape[0]
    groups, slots = nodes // TILE, send_list.shape[0] // SLOT
    ext = blocks + 2 * BORDER
    width = (ext + LAT - 1) // LAT * LAT
    vmem = pl.BlockSpec(memory_space=pltpu.VMEM)
    specs = [vmem] * 12
    specs[2] = pl.BlockSpec(memory_space=pl.ANY)
    specs[5] = pl.BlockSpec(memory_space=pltpu.SMEM)
    return tuple(
        pl.pallas_call(
            functools.partial(kernel, levels),
            out_shape=(
                jax.ShapeDtypeStruct(fine_nodes.shape, BF16),
                jax.ShapeDtypeStruct(coarse_nodes.shape, BF16),
            ),
            in_specs=specs,
            out_specs=(vmem, vmem),
            scratch_shapes=[
                pltpu.VMEM((edges, LAT), BF16),
                pltpu.VMEM(((groups + slots // 2) * LAT, TILE), BF16),
                pltpu.VMEM((groups * LAT, TILE), BF16),
                pltpu.VMEM((slots, LAT, SLOT), BF16),
                pltpu.VMEM((slots, LAT, SLOT), BF16),
                pltpu.VMEM((width, LAT), BF16),
                pltpu.VMEM((nodes, width), BF16),
                pltpu.VMEM((width, nodes), BF16),
                pltpu.VMEM((nodes, LAT), F32),
                pltpu.VMEM((nodes, LAT), F32),
                pltpu.VMEM((nodes, LAT), BF16),
                pltpu.VMEM((ext, LAT), BF16),
                pltpu.VMEM((2, 2 * BORDER, LAT), BF16),
                pltpu.VMEM((groups * LAT, TILE), F32),
                pltpu.VMEM((3 * LAT, LAT), BF16),
                pltpu.VMEM((LAT, LAT), F32),
                pltpu.SemaphoreType.DMA,
                pltpu.SemaphoreType.DMA((7,)),
                pltpu.SemaphoreType.DMA((7,)),
            ],
            compiler_params=pltpu.CompilerParams(collective_id=0, has_side_effects=True),
            name="graph_step",
        )(
            fine_nodes,
            coarse_nodes,
            edge_latents,
            senders.reshape(-1, LAT),
            receivers.reshape(-1, LAT),
            live_blocks,
            send_list.reshape(-1, SLOT),
            parents.reshape(-1, LAT),
            edge_weight,
            node_weights,
            out_weights,
            gains,
        )
    )


def solution(mesh):
    both = ("region", "level")
    in_specs = (
        P(both, None),
        P(both, None),
        P(both, None),
        P(both),
        P(both),
        P(both),
        P(both),
        P(both),
        P(),
        P(),
        P(),
        P(),
    )
    return jax.shard_map(
        functools.partial(body, mesh.shape["level"]),
        mesh=mesh,
        in_specs=in_specs,
        out_specs=(P(both, None), P(both, None)),
        check_vma=False,
    )
```

time: 156 us -> 47.5 us (0.30)
  the two profiles are of different devices: /device:TPU:126 before, /device:TPU:128 now
where the time goes in v1:
time: 47.5 us; the launch traced here: 47.3 us
  Pallas kernels  42.8 us (90%)
  local copies, waits for them, and re-layouts  3.24 us (7%)
  between operations  1.29 us (3%)
    pallas_call x1, Pallas kernels, body(): pl.pallas_call(functools.partial(kernel, levels), out_shape=(jax.ShapeDty...  42.8 us
    unnamed x2, local copies, waits for them, and re-layouts  3.24 us

profile of v1, /device:TPU:128, one launch (start us, length us, event | category | flops | bytes accessed | tf_op | source)
XLA Modules:
  0.0 47.3 jit_solution(17368280309173733148)
XLA Ops:
  1.3 42.8 %graph_step.1 = (bf16[1280,128]{1,0:T(8,128)(2,1)}, bf16[320,128]{1,0:T(8,128)(2,1)}) custom-call(bf16[1280,128]{1,0:T(8,128)(2,1)} %fine.1, bf16[320,128]{1,0:T(8,128)(2,1)} %coarse.1, bf16[8192,128]{1,0:T(8,128)(2,1)} %latents.1, s32[64,128]{1,0:T(8,128)} %bitcast.4, s32[64,128]{1,0:T(8,128)} %bitcast.5, s32[1]{0:T(128)S(6)} %copy.16.live, ...), custom_call_target="tpu_custom_call" | custom-call | tf_op jit(solution)/shard_map/graph_step/pallas_call | solution.py:352
  44.1 1.7 %copy.17 = bf16[1280,128]{1,0:T(8,128)(2,1)} copy(bf16[1280,128]{1,0:T(8,128)(2,1)} %get-tuple-element.4) | data formatting | bytes 655360
  45.8 1.5 %copy.18 = bf16[320,128]{1,0:T(8,128)(2,1)} copy(bf16[320,128]{1,0:T(8,128)(2,1)} %get-tuple-element.5) | data formatting | bytes 163840

commit v2 on v1

v2 whole, which is shorter than its diff:
```python
import functools

import jax
import jax.numpy as jnp
from jax import lax
from jax.experimental import pallas as pl
from jax.experimental.pallas import tpu as pltpu
from jax.sharding import PartitionSpec as P

MESH = pl.DeviceIdType.MESH
F32 = jnp.float32
BF16 = jnp.bfloat16
I32 = jnp.int32
LAT = 128
HALF = LAT // 2
BORDER = 64
EDGE_ROWS = 4 * BORDER
SLOT = 128
norm_eps = 1e-05
group_edges = 1024
sub = group_edges // LAT
TILE = 256
ahead = 2
lane_tiles = 4
top = 16380.0


def dot(a, b, ca=1, cb=0):
    return lax.dot_general(a, b, (((ca,), (cb,)), ((), ())), preferred_element_type=F32)


def half_silu(h):
    return (h * jnp.tanh(h) + h).astype(BF16)


def scale_rows(c):
    return c * lax.rsqrt(jnp.mean(c * c, axis=1, keepdims=True) + norm_eps)


def hot_columns(ids, rows):
    low, high = (ids & (TILE - 1)).astype(F32), ids >> 8
    shape = (TILE, ids.shape[1])
    place = lax.broadcasted_iota(I32, shape, 0).astype(BF16)
    parts = []
    for g in range(rows // TILE):
        mine = jnp.where(high == g, low, -1.0).astype(BF16)
        parts.append(
            jnp.where(place == jnp.broadcast_to(mine, shape), jnp.ones((), BF16), jnp.zeros((), BF16))
        )
    return jnp.concatenate(parts, axis=0)


def split(x, axis):
    high = x.astype(BF16)
    return jnp.concatenate([high, (x - high.astype(F32)).astype(BF16)], axis=axis)


def centered(w):
    wide = w.astype(F32)
    return split(wide - jnp.mean(wide, axis=1, keepdims=True), 0)


def twice(x, axis=1):
    return jnp.concatenate([x, x], axis=axis)


def kernel(
    levels,
    fine_h,
    coarse_h,
    latents_h,
    senders_h,
    receivers_h,
    live_h,
    send_list_h,
    parents_h,
    edge_w_h,
    node_w_h,
    out_w_h,
    gains_h,
    mid,
    down_pre,
    par_edge,
    base_edge,
    total_edge,
    new_inner,
    late_w,
    late_out,
    late_gain,
    fine,
    coarse,
    latents,
    senders,
    receivers,
    live,
    send_list,
    parents,
    edge_w,
    node_w,
    out_w,
    gains,
    table,
    full,
    sender_q,
    receiver_q,
    packed,
    acts,
    outgoing,
    arrived,
    cext,
    par_inner,
    par_cols,
    up_pre,
    sums_out,
    sums_in,
    acc,
    first_t,
    second_t,
    gain_t,
    scale_t,
    load_sem,
    send_sem,
    recv_sem,
):
    r, l = lax.axis_index("region"), lax.axis_index("level")
    nodes, blocks = fine.shape[0], coarse.shape[0]
    inner = blocks - 2 * BORDER
    ext = blocks + 2 * BORDER
    groups = nodes // TILE
    slots = arrived.shape[0]
    edge_blocks = latents.shape[0] // group_edges
    has_lower, has_upper = l > 0, l < levels - 1
    lower, upper, peer = (r, l - 1), (r, l + 1), (1 - r, l)

    barrier = pltpu.get_barrier_semaphore()
    pl.semaphore_signal(barrier, inc=1, device_id=peer, device_id_type=MESH)

    @pl.when(has_lower)
    def _():
        pl.semaphore_signal(barrier, inc=1, device_id=lower, device_id_type=MESH)

    @pl.when(has_upper)
    def _():
        pl.semaphore_signal(barrier, inc=1, device_id=upper, device_id_type=MESH)

    pairs = [
        (edge_w_h, edge_w),
        (fine_h, fine),
        (send_list_h, send_list),
        (coarse_h, coarse),
        (receivers_h, receivers),
        (senders_h, senders),
        (parents_h, parents),
        (latents_h, latents),
        (out_w_h, out_w),
        (gains_h, gains),
        (node_w_h, node_w),
        (live_h, live),
    ]
    loads = [pltpu.make_async_copy(s, d, load_sem.at[k]) for k, (s, d) in enumerate(pairs)]
    for load in loads:
        load.start()

    def remote(kind, src, dst, device):
        return pltpu.make_async_remote_copy(
            src_ref=src,
            dst_ref=dst,
            send_sem=send_sem.at[kind],
            recv_sem=recv_sem.at[kind],
            device_id=device,
            device_id_type=MESH,
        )

    halo_down = remote(0, outgoing.at[0], arrived.at[1], lower)
    halo_up = remote(1, outgoing.at[1], arrived.at[0], upper)
    halo_peer = remote(2, outgoing.at[3 - r], arrived.at[2 + r], peer)
    coarse_down = remote(3, coarse.at[pl.ds(0, BORDER)], cext.at[pl.ds(3 * BORDER, BORDER)], lower)
    coarse_up = remote(4, coarse.at[pl.ds(blocks - BORDER, BORDER)], cext.at[pl.ds(0, BORDER)], upper)
    sums_down = remote(5, sums_out.at[0], sums_in.at[1], lower)
    sums_up = remote(6, sums_out.at[1], sums_in.at[0], upper)

    loads[0].wait()
    w_both = jnp.concatenate(
        [
            (edge_w[LAT : 2 * LAT, :].astype(F32) * 0.5).T.astype(BF16),
            (edge_w[2 * LAT :, :].astype(F32) * 0.5).T.astype(BF16),
        ],
        axis=0,
    )
    loads[1].wait()
    for g in range(groups):
        both = dot(w_both, fine[g * TILE : (g + 1) * TILE, :], 1, 1)
        full[:, g * TILE : (g + 1) * TILE] = both
        table[:, g * TILE : (g + 1) * TILE] = both[:LAT].astype(BF16)

    loads[2].wait()
    sends = jnp.concatenate([send_list[j : j + 1, :] for j in range(slots)], axis=1)
    picked = dot(table[:, :nodes], hot_columns(sends, nodes)).astype(BF16)
    for j in range(slots):
        outgoing[j] = picked[:, j * SLOT : (j + 1) * SLOT]
    loads[3].wait()

    pl.semaphore_wait(barrier, 1 + has_lower.astype(I32) + has_upper.astype(I32))

    @pl.when(has_lower)
    def _():
        halo_down.start()

    @pl.when(has_upper)
    def _():
        halo_up.start()

    halo_peer.start()

    @pl.when(has_lower)
    def _():
        coarse_down.start()

    @pl.when(has_upper)
    def _():
        coarse_up.start()

    arrived[2 + r] = outgoing[2 + r]
    cext[BORDER : 2 * BORDER, :] = coarse[:BORDER, :]
    cext[2 * BORDER : 3 * BORDER, :] = coarse[blocks - BORDER :, :]
    cext[EDGE_ROWS : EDGE_ROWS + inner, :] = coarse[BORDER : blocks - BORDER, :]
    cext[EDGE_ROWS + inner :, :] = jnp.zeros((cext.shape[0] - EDGE_ROWS - inner, LAT), BF16)

    @pl.when(jnp.logical_not(has_lower))
    def _():
        arrived[0] = jnp.zeros((LAT, SLOT), BF16)
        cext[:BORDER, :] = jnp.zeros((BORDER, LAT), BF16)
        sums_in[0] = jnp.zeros((2 * BORDER, LAT), BF16)

    @pl.when(jnp.logical_not(has_upper))
    def _():
        arrived[1] = jnp.zeros((LAT, SLOT), BF16)
        cext[3 * BORDER : 4 * BORDER, :] = jnp.zeros((BORDER, LAT), BF16)
        sums_in[1] = jnp.zeros((2 * BORDER, LAT), BF16)

    most = jnp.max(jnp.abs(full[...]), axis=1, keepdims=True)
    most = jnp.maximum(jnp.maximum(most[:LAT], most[LAT:]), 1e-30)
    step = most * (1.0 / top)
    scale_t[...] = jnp.broadcast_to(step * (1.0 / 65536.0), (LAT, LAT))
    inverse = top / most

    def pack(start, count, target):
        for t in range(count):
            cols = slice(t * LAT, (t + 1) * LAT)
            q = full[start : start + LAT, cols] * inverse
            low = jnp.round(q[HALF:])
            high = jnp.round(q[:HALF] - low * (1.0 / 65536.0))
            target[:, cols] = high.astype(I32) * 65536 + low.astype(I32)

    pack(0, lane_tiles, sender_q)
    pack(LAT, nodes // LAT, receiver_q)

    def gather(b):
        for j in range(sub):

            def look_up(ids, target, x, count):
                low = jnp.broadcast_to(ids & (LAT - 1), (HALF, LAT))
                high = jnp.broadcast_to(ids >> 7, (HALF, LAT))
                for t in range(count):
                    found = jnp.take_along_axis(target[:, t * LAT : (t + 1) * LAT], low, axis=1)
                    x = found if x is None else jnp.where(high == t, found, x)
                return x

            s, t = senders[pl.ds(b * sub + j, 1), :], receivers[pl.ds(b * sub + j, 1), :]
            total = look_up(t, receiver_q, None, nodes // LAT)
            total = total + look_up(s, sender_q, jnp.zeros((HALF, LAT), I32), lane_tiles)
            packed[b, :, j * LAT : (j + 1) * LAT] = total

    loads[4].wait()
    loads[5].wait()

    def gather_step(b, carry):
        gather(b)
        return carry

    lax.fori_loop(0, ahead, gather_step, 0)

    loads[6].wait()
    offset = BORDER - l * blocks
    for j in range(nodes // LAT):
        p = parents[j : j + 1, :] + offset
        p = jnp.where(
            p < 2 * BORDER, p, jnp.where(p < 2 * BORDER + inner, p + 2 * BORDER, p - inner)
        )
        par_cols[:, j * LAT : (j + 1) * LAT] = hot_columns(p, par_cols.shape[0])
        column = jnp.broadcast_to(p.astype(F32), (LAT, LAT)).T
        ids = lax.broadcasted_iota(I32, (LAT, LAT), 1).astype(F32)
        rows = slice(j * LAT, (j + 1) * LAT)
        for k in range(2):
            cols = slice(k * LAT, (k + 1) * LAT)
            par_edge[rows, cols] = jnp.where(ids + float(k * LAT) == column, 1.0, 0.0).astype(BF16)
            par_inner[rows, cols] = jnp.where(
                ids + float(EDGE_ROWS + k * LAT) == column, 1.0, 0.0
            ).astype(BF16)

    for k in range(7, 12):
        loads[k].wait()
    first_t[:LAT, :] = (edge_w[:LAT, :].astype(F32) * 0.5).T.astype(BF16)
    eye = lax.broadcasted_iota(I32, (LAT, LAT), 0) == lax.broadcasted_iota(I32, (LAT, LAT), 1)
    first_t[LAT:, :] = jnp.where(eye, 1.0, 0.0).astype(BF16)
    wide = out_w[0].astype(F32).T
    second_t[...] = split(wide - jnp.mean(wide, axis=0, keepdims=True), 1)
    gain_t[...] = jnp.broadcast_to(gains[0:1, :], (LAT, LAT)).T
    acc[...] = jnp.zeros_like(acc)
    late_w[...] = node_w[2:4]
    late_out[0] = centered(out_w[3])
    late_out[1] = centered(out_w[4])
    late_gain[...] = gains[...]

    halo_peer.wait()

    @pl.when(has_lower)
    def _():
        halo_down.wait_send()
        halo_up.wait_recv()
        coarse_down.wait_send()
        coarse_up.wait_recv()

    @pl.when(has_upper)
    def _():
        halo_up.wait_send()
        halo_down.wait_recv()
        coarse_up.wait_send()
        coarse_down.wait_recv()

    for j in range(slots):
        table[:, nodes + j * SLOT : nodes + (j + 1) * SLOT] = arrived[j]

    gain_all = jnp.concatenate([gain_t[...]] * sub, axis=1)
    scale_all = jnp.concatenate([scale_t[...]] * sub, axis=1)
    skip = lane_tiles * LAT
    listed = table.shape[1]

    def row(ref, b):
        return jnp.concatenate([ref[pl.ds(b * sub + j, 1), :] for j in range(sub)], axis=1)

    def block(b):
        return latents[pl.ds(pl.multiple_of(b * group_edges, group_edges), group_edges), :]

    def hidden_layer(b):
        h = dot(first_t[:LAT, :], block(b), 1, 1)
        h = h + dot(table[:, skip:], hot_columns(row(senders, b) - skip, listed - skip))
        own = packed[b]
        own = jnp.concatenate([own.astype(F32), (own << 16).astype(F32)], axis=0)
        acts[b] = half_silu(h + own * scale_all)

    def add_edges(b):
        lat = dot(first_t[LAT:, :], block(b), 1, 1)
        c = dot(second_t[...], twice(acts[b], 0))
        spread = lax.rsqrt(jnp.mean(c * c, axis=0, keepdims=True) + norm_eps)
        updated = (lat + c * spread * gain_all).astype(BF16)
        ids = row(receivers, b)
        position = b * group_edges + lax.broadcasted_iota(I32, (1, group_edges), 1)
        target = jnp.where(position < live[0] * 128, ids >> 8, groups)
        masked = jnp.concatenate(
            [
                updated
                * jnp.broadcast_to(jnp.where(target == g, 1.0, 0.0).astype(BF16), updated.shape)
                for g in range(groups)
            ],
            axis=0,
        )
        acc[...] += dot(masked, hot_columns(ids & (TILE - 1), TILE), 1, 1)

    hidden_layer(0)

    def full_step(b, carry):
        add_edges(b)
        hidden_layer(b + 1)
        gather(b + ahead)
        return carry

    def last_step(b, carry):
        add_edges(b)
        hidden_layer(b + 1)
        return carry

    lax.fori_loop(0, edge_blocks - ahead, full_step, 0)
    lax.fori_loop(edge_blocks - ahead, edge_blocks - 1, last_step, 0)
    add_edges(edge_blocks - 1)

    up_table = split(dot(cext[...], node_w[1, LAT:, :]), 1)
    for g in range(groups):
        rows = slice(g * TILE, (g + 1) * TILE)
        found = dot(par_edge[rows, :], up_table[:TILE]) + dot(par_inner[rows, :], up_table[TILE:])
        up_pre[rows, :] = found[:, :LAT] + found[:, LAT:]

    fine_out_w, up_out_w = centered(out_w[1]), centered(out_w[2])
    sums = jnp.zeros((cext.shape[0], 2 * LAT), F32)
    for g in range(groups):
        rows = slice(g * TILE, (g + 1) * TILE)
        own = fine[rows, :]
        agg = acc[g * LAT : (g + 1) * LAT, :].T.astype(BF16)
        h = dot(jnp.concatenate([own, agg], axis=1), node_w[0])
        new = scale_rows(dot(twice(half_silu(0.5 * h)), fine_out_w)) * gains[1:2, :]
        new = (own.astype(F32) + new).astype(BF16)
        mid[rows, :] = new
        h = dot(new, node_w[1, :LAT, :]) + up_pre[rows, :]
        upward = scale_rows(dot(twice(half_silu(0.5 * h)), up_out_w)) * gains[2:3, :]
        sums = sums + dot(par_cols[:, rows], split(upward, 1))
    sums = sums[:, :LAT] + sums[:, LAT:]
    sums_out[0] = sums[: 2 * BORDER].astype(BF16)
    sums_out[1] = sums[2 * BORDER : EDGE_ROWS].astype(BF16)

    @pl.when(has_lower)
    def _():
        sums_down.start()

    @pl.when(has_upper)
    def _():
        sums_up.start()

    base = cext[EDGE_ROWS:, :]
    h = dot(jnp.concatenate([base, sums[EDGE_ROWS:].astype(BF16)], axis=1), node_w[2])
    new = scale_rows(dot(twice(half_silu(0.5 * h)), late_out[0])) * gains[3:4, :]
    new = (base.astype(F32) + new).astype(BF16)
    new_inner[...] = new[:inner]
    inner_table = split(dot(new, node_w[3, LAT:, :]), 1)
    for g in range(groups):
        rows = slice(g * TILE, (g + 1) * TILE)
        found = dot(par_inner[rows, :], inner_table)
        down_pre[rows, :] = dot(mid[rows, :], node_w[3, :LAT, :]) + (found[:, :LAT] + found[:, LAT:])
    base_edge[...] = cext[:EDGE_ROWS, :]

    @pl.when(has_lower)
    def _():
        sums_down.wait_send()
        sums_up.wait_recv()

    @pl.when(has_upper)
    def _():
        sums_up.wait_send()
        sums_down.wait_recv()

    total_edge[: 2 * BORDER, :] = (sums[: 2 * BORDER] + sums_in[0].astype(F32)).astype(BF16)
    total_edge[2 * BORDER :, :] = (sums[2 * BORDER : EDGE_ROWS] + sums_in[1].astype(F32)).astype(BF16)


def finish(
    mid,
    down_pre,
    par_edge,
    base_edge,
    total_edge,
    new_inner,
    late_w,
    late_out,
    late_gain,
    fine_out,
    coarse_out,
    fine_v,
    coarse_v,
    sem,
):
    nodes, blocks = fine_v.shape[0], coarse_v.shape[0]
    base = base_edge[...]
    h = dot(jnp.concatenate([base, total_edge[...]], axis=1), late_w[0])
    new = scale_rows(dot(twice(half_silu(0.5 * h)), late_out[0])) * late_gain[3:4, :]
    new = (base.astype(F32) + new).astype(BF16)
    coarse_v[:BORDER, :] = new[BORDER : 2 * BORDER]
    coarse_v[blocks - BORDER :, :] = new[2 * BORDER : 3 * BORDER]
    coarse_v[BORDER : blocks - BORDER, :] = new_inner[...]
    copies = [pltpu.make_async_copy(coarse_v, coarse_out, sem.at[nodes // TILE])]
    copies[0].start()
    edge_table = split(dot(new, late_w[1, LAT:, :]), 1)
    for g in range(nodes // TILE):
        rows = slice(g * TILE, (g + 1) * TILE)
        found = dot(par_edge[rows, :], edge_table)
        h = down_pre[rows, :] + (found[:, :LAT] + found[:, LAT:])
        new = scale_rows(dot(twice(half_silu(0.5 * h)), late_out[1])) * late_gain[4:5, :]
        fine_v[rows, :] = (mid[rows, :].astype(F32) + new).astype(BF16)
        part = pl.ds(g * TILE, TILE)
        copies.append(pltpu.make_async_copy(fine_v.at[part], fine_out.at[part], sem.at[g]))
        copies[-1].start()
    for copy in copies:
        copy.wait()


def body(
    levels,
    fine_nodes,
    coarse_nodes,
    edge_latents,
    senders,
    receivers,
    live_blocks,
    send_list,
    parents,
    edge_weight,
    node_weights,
    out_weights,
    gains,
):
    arrays = (
        fine_nodes,
        coarse_nodes,
        edge_latents,
        senders.reshape(-1, LAT),
        receivers.reshape(-1, LAT),
        live_blocks,
        send_list.reshape(-1, SLOT),
        parents.reshape(-1, LAT),
        edge_weight,
        node_weights,
        out_weights,
        gains,
    )
    nodes, blocks, edges = fine_nodes.shape[0], coarse_nodes.shape[0], edge_latents.shape[0]
    groups, slots = nodes // TILE, send_list.shape[0] // SLOT
    inner = blocks - 2 * BORDER
    hbm = pl.BlockSpec(memory_space=pltpu.HBM)
    vmem = pl.BlockSpec(memory_space=pltpu.VMEM)
    held = [pltpu.VMEM(a.shape, a.dtype) for a in arrays]
    held[5] = pltpu.SMEM((1,), I32)
    edge_blocks = edges // group_edges
    state = pl.pallas_call(
        functools.partial(kernel, levels),
        out_shape=(
            pltpu.VMEM((nodes, LAT), BF16),
            pltpu.VMEM((nodes, LAT), F32),
            pltpu.VMEM((nodes, TILE), BF16),
            pltpu.VMEM((EDGE_ROWS, LAT), BF16),
            pltpu.VMEM((EDGE_ROWS, LAT), BF16),
            pltpu.VMEM((inner, LAT), BF16),
            pltpu.VMEM((2, 2 * LAT, LAT), BF16),
            pltpu.VMEM((2, 2 * LAT, LAT), BF16),
            pltpu.VMEM(gains.shape, F32),
        ),
        in_specs=[hbm] * 12,
        out_specs=(vmem,) * 9,
        scratch_shapes=held
        + [
            pltpu.VMEM((LAT, nodes + slots * SLOT), BF16),
            pltpu.VMEM((2 * LAT, nodes), F32),
            pltpu.VMEM((HALF, lane_tiles * LAT), I32),
            pltpu.VMEM((HALF, nodes), I32),
            pltpu.VMEM((edge_blocks, HALF, group_edges), I32),
            pltpu.VMEM((edge_blocks, LAT, group_edges), BF16),
            pltpu.VMEM((slots, LAT, SLOT), BF16),
            pltpu.VMEM((slots, LAT, SLOT), BF16),
            pltpu.VMEM((2 * TILE, LAT), BF16),
            pltpu.VMEM((nodes, TILE), BF16),
            pltpu.VMEM((2 * TILE, nodes), BF16),
            pltpu.VMEM((nodes, LAT), F32),
            pltpu.VMEM((2, 2 * BORDER, LAT), BF16),
            pltpu.VMEM((2, 2 * BORDER, LAT), BF16),
            pltpu.VMEM((groups * LAT, TILE), F32),
            pltpu.VMEM((2 * LAT, LAT), BF16),
            pltpu.VMEM((LAT, 2 * LAT), BF16),
            pltpu.VMEM((LAT, LAT), F32),
            pltpu.VMEM((LAT, LAT), F32),
            pltpu.SemaphoreType.DMA((12,)),
            pltpu.SemaphoreType.DMA((7,)),
            pltpu.SemaphoreType.DMA((7,)),
        ],
        compiler_params=pltpu.CompilerParams(
            collective_id=0, has_side_effects=True, vmem_limit_bytes=64_600_000
        ),
        name="graph_step",
    )(*arrays)
    return pl.pallas_call(
        finish,
        out_shape=(
            jax.ShapeDtypeStruct(fine_nodes.shape, BF16),
            jax.ShapeDtypeStruct(coarse_nodes.shape, BF16),
        ),
        in_specs=[vmem] * 9,
        out_specs=(hbm, hbm),
        scratch_shapes=[
            pltpu.VMEM(fine_nodes.shape, BF16),
            pltpu.VMEM(coarse_nodes.shape, BF16),
            pltpu.SemaphoreType.DMA((groups + 1,)),
        ],
        compiler_params=pltpu.CompilerParams(vmem_limit_bytes=16 * 1024 * 1024),
        name="graph_finish",
    )(*state)


def solution(mesh):
    both = ("region", "level")
    in_specs = (
        P(both, None),
        P(both, None),
        P(both, None),
        P(both),
        P(both),
        P(both),
        P(both),
        P(both),
        P(),
        P(),
        P(),
        P(),
    )
    return jax.shard_map(
        functools.partial(body, mesh.shape["level"]),
        mesh=mesh,
        in_specs=in_specs,
        out_specs=(P(both, None), P(both, None)),
        check_vma=False,
    )
```

time: 47.5 us -> 32.6 us (0.69)
  Pallas kernels: 42.8 us -> 31.2 us
  local copies, waits for them, and re-layouts: 3.24 us -> 0 us
    pallas_call x1 -> x2, Pallas kernels: 42.8 us -> 31.2 us  [the longest x1 29.3 us: body(): pl.pallas_call(functools.partial(kernel, levels), out_shape=(pltpu.VMEM((...]
    unnamed x2 -> x0, local copies, waits for them, and re-layouts: 3.24 us -> none
where the time goes in v2:
time: 32.6 us; the launch traced here: 32.5 us
  Pallas kernels  31.2 us (96%)
  between operations  1.29 us (4%)
    pallas_call x1, Pallas kernels, body(): pl.pallas_call(functools.partial(kernel, levels), out_shape=(pltpu.VMEM((...  29.3 us
    pallas_call x1, Pallas kernels, body(): pl.pallas_call(finish, out_shape=(jax.ShapeDtypeStruct(fine_nodes.shape,...  1.92 us

profile of v2, /device:TPU:128, one launch (start us, length us, event | category | flops | bytes accessed | tf_op | source)
XLA Modules:
  0.0 32.5 jit_solution(12622185860680111529)
XLA Ops:
  1.3 29.3 %graph_step.1 = (bf16[1280,128]{1,0:T(8,128)(2,1)S(1)}, f32[1280,128]{1,0:T(8,128)S(1)}, bf16[1280,256]{1,0:T(8,128)(2,1)S(1)}, bf16[256,128]{1,0:T(8,128)(2,1)S...) custom-call(bf16[1280,128]{1,0:T(8,128)(2,1)} %fine_h.1, ...), custom_call_target="tpu_custom_call" | custom-call | tf_op jit(solution)/shard_map/graph_step/pallas_call | solution.py:521
  30.6 1.9 %graph_finish.1 = (bf16[1280,128]{1,0:T(8,128)(2,1)}, bf16[320,128]{1,0:T(8,128)(2,1)}) custom-call(bf16[1280,128]{1,0:T(8,128)(2,1)S(1)} %get-tuple-element.11.mid, f32[1280,128]{1,0:T(8,128)S(1)} %get-tuple-element.12.down_pre, bf16[1280,256]{1,0:T(8,128)(2,1)S(1)} %get-tuple-element.13.par_edge, bf16[256,128]{1,0:T(8,128)(2,1)S(1)} %get-tuple-element.14.base_edge, ...), custom_call_target="tpu_custom_call" | custom-call | tf_op jit(solution)/shard_map/graph_finish/pallas_call | solution.py:566

commit v3 on v2

--- a/solution.py
+++ b/solution.py
@@ -109,6 +109,7 @@
     arrived,
     cext,
     par_inner,
+    par_near,
     par_cols,
     up_pre,
     sums_out,
@@ -297,6 +298,8 @@
             par_inner[rows, cols] = jnp.where(
                 ids + float(EDGE_ROWS + k * LAT) == column, 1.0, 0.0
             ).astype(BF16)
+        near = jnp.where(ids < float(BORDER), ids, ids + float(2 * BORDER))
+        par_near[rows, :] = jnp.where(near == column, 1.0, 0.0).astype(BF16)
 
     for k in range(7, 12):
         loads[k].wait()
@@ -311,6 +314,15 @@
     late_out[0] = centered(out_w[3])
     late_out[1] = centered(out_w[4])
     late_gain[...] = gains[...]
+
+    none = jnp.zeros((BORDER, LAT), BF16)
+    own_edge = jnp.concatenate([none, coarse[:BORDER, :], coarse[blocks - BORDER :, :], none], axis=0)
+    edge_table = split(dot(own_edge, node_w[1, LAT:, :]), 1)
+    inner_table = split(dot(cext[EDGE_ROWS:, :], node_w[1, LAT:, :]), 1)
+    for g in range(groups):
+        rows = slice(g * TILE, (g + 1) * TILE)
+        found = dot(par_edge[rows, :], edge_table) + dot(par_inner[rows, :], inner_table)
+        up_pre[rows, :] = found[:, :LAT] + found[:, LAT:]
 
     halo_peer.wait()
 
@@ -384,25 +396,29 @@
     lax.fori_loop(edge_blocks - ahead, edge_blocks - 1, last_step, 0)
     add_edges(edge_blocks - 1)
 
-    up_table = split(dot(cext[...], node_w[1, LAT:, :]), 1)
-    for g in range(groups):
-        rows = slice(g * TILE, (g + 1) * TILE)
-        found = dot(par_edge[rows, :], up_table[:TILE]) + dot(par_inner[rows, :], up_table[TILE:])
-        up_pre[rows, :] = found[:, :LAT] + found[:, LAT:]
-
     fine_out_w, up_out_w = centered(out_w[1]), centered(out_w[2])
-    sums = jnp.zeros((cext.shape[0], 2 * LAT), F32)
-    for g in range(groups):
-        rows = slice(g * TILE, (g + 1) * TILE)
-        own = fine[rows, :]
-        agg = acc[g * LAT : (g + 1) * LAT, :].T.astype(BF16)
-        h = dot(jnp.concatenate([own, agg], axis=1), node_w[0])
-        new = scale_rows(dot(twice(half_silu(0.5 * h)), fine_out_w)) * gains[1:2, :]
-        new = (own.astype(F32) + new).astype(BF16)
-        mid[rows, :] = new
-        h = dot(new, node_w[1, :LAT, :]) + up_pre[rows, :]
-        upward = scale_rows(dot(twice(half_silu(0.5 * h)), up_out_w)) * gains[2:3, :]
-        sums = sums + dot(par_cols[:, rows], split(upward, 1))
+    near = jnp.concatenate([cext[:BORDER, :], cext[3 * BORDER : EDGE_ROWS, :]], axis=0)
+    near_table = dot(near, node_w[1, LAT:, :]).astype(BF16)
+    up_w = jnp.concatenate([node_w[1, :LAT, :], near_table], axis=0)
+    parts = [slice(g * TILE, (g + 1) * TILE) for g in range(groups)]
+    aggs = [acc[g * LAT : (g + 1) * LAT, :].T.astype(BF16) for g in range(groups)]
+    hs = [
+        dot(jnp.concatenate([fine[p, :], agg], axis=1), node_w[0]) for p, agg in zip(parts, aggs)
+    ]
+    cs = [dot(twice(half_silu(0.5 * h)), fine_out_w) for h in hs]
+    news = [
+        (fine[p, :].astype(F32) + scale_rows(c) * gains[1:2, :]).astype(BF16)
+        for p, c in zip(parts, cs)
+    ]
+    for p, new in zip(parts, news):
+        mid[p, :] = new
+    hs = [
+        dot(jnp.concatenate([new, par_near[p, :]], axis=1), up_w) + up_pre[p, :]
+        for p, new in zip(parts, news)
+    ]
+    cs = [dot(twice(half_silu(0.5 * h)), up_out_w) for h in hs]
+    ups = jnp.concatenate([split(scale_rows(c) * gains[2:3, :], 1) for c in cs], axis=0)
+    sums = dot(par_cols[...], ups)
     sums = sums[:, :LAT] + sums[:, LAT:]
     sums_out[0] = sums[: 2 * BORDER].astype(BF16)
     sums_out[1] = sums[2 * BORDER : EDGE_ROWS].astype(BF16)
@@ -468,12 +484,14 @@
     copies = [pltpu.make_async_copy(coarse_v, coarse_out, sem.at[nodes // TILE])]
     copies[0].start()
     edge_table = split(dot(new, late_w[1, LAT:, :]), 1)
-    for g in range(nodes // TILE):
-        rows = slice(g * TILE, (g + 1) * TILE)
-        found = dot(par_edge[rows, :], edge_table)
-        h = down_pre[rows, :] + (found[:, :LAT] + found[:, LAT:])
-        new = scale_rows(dot(twice(half_silu(0.5 * h)), late_out[1])) * late_gain[4:5, :]
-        fine_v[rows, :] = (mid[rows, :].astype(F32) + new).astype(BF16)
+    parts = [slice(g * TILE, (g + 1) * TILE) for g in range(nodes // TILE)]
+    found = [dot(par_edge[p, :], edge_table) for p in parts]
+    hs = [down_pre[p, :] + (f[:, :LAT] + f[:, LAT:]) for p, f in zip(parts, found)]
+    cs = [dot(twice(half_silu(0.5 * h)), late_out[1]) for h in hs]
+    for g, c in enumerate(cs):
+        p = parts[g]
+        new = scale_rows(c) * late_gain[4:5, :]
+        fine_v[p, :] = (mid[p, :].astype(F32) + new).astype(BF16)
         part = pl.ds(g * TILE, TILE)
         copies.append(pltpu.make_async_copy(fine_v.at[part], fine_out.at[part], sem.at[g]))
         copies[-1].start()
@@ -545,6 +563,7 @@
             pltpu.VMEM((slots, LAT, SLOT), BF16),
             pltpu.VMEM((2 * TILE, LAT), BF16),
             pltpu.VMEM((nodes, TILE), BF16),
+            pltpu.VMEM((nodes, 2 * BORDER), BF16),
             pltpu.VMEM((2 * TILE, nodes), BF16),
             pltpu.VMEM((nodes, LAT), F32),
             pltpu.VMEM((2, 2 * BORDER, LAT), BF16),

time: 32.6 us -> 31.5 us (0.966)
  Pallas kernels: 31.2 us -> 30.1 us
    pallas_call x1, Pallas kernels: 29.3 us -> 28.2 us  [body(): pl.pallas_call(functools.partial(kernel, levels), out_shape=(pltpu.VMEM((...]
where the time goes in v3:
time: 31.5 us; the launch traced here: 31.3 us
  Pallas kernels  30.1 us (96%)
  between operations  1.29 us (4%)
    pallas_call x1, Pallas kernels, body(): pl.pallas_call(functools.partial(kernel, levels), out_shape=(pltpu.VMEM((...  28.2 us
    pallas_call x1, Pallas kernels, body(): pl.pallas_call(finish, out_shape=(jax.ShapeDtypeStruct(fine_nodes.shape,...  1.82 us

profile of v3, /device:TPU:128, one launch (start us, length us, event | category | flops | bytes accessed | tf_op | source)
XLA Modules:
  0.0 31.3 jit_solution(2248414550619885415)
XLA Ops:
  1.3 28.2 %graph_step.1 = (bf16[1280,128]{1,0:T(8,128)(2,1)S(1)}, f32[1280,128]{1,0:T(8,128)S(1)}, bf16[1280,256]{1,0:T(8,128)(2,1)S(1)}, bf16[256,128]{1,0:T(8,128)(2,1)S...) custom-call(bf16[1280,128]{1,0:T(8,128)(2,1)} %fine_h.1, ...), custom_call_target="tpu_custom_call" | custom-call | tf_op jit(solution)/shard_map/graph_step/pallas_call | solution.py:539
  29.5 1.8 %graph_finish.1 = (bf16[1280,128]{1,0:T(8,128)(2,1)}, bf16[320,128]{1,0:T(8,128)(2,1)}) custom-call(bf16[1280,128]{1,0:T(8,128)(2,1)S(1)} %get-tuple-element.11.mid, f32[1280,128]{1,0:T(8,128)S(1)} %get-tuple-element.12.down_pre, bf16[1280,256]{1,0:T(8,128)(2,1)S(1)} %get-tuple-element.13.par_edge, bf16[256,128]{1,0:T(8,128)(2,1)S(1)} %get-tuple-element.14.base_edge, ...), custom_call_target="tpu_custom_call" | custom-call | tf_op jit(solution)/shard_map/graph_finish/pallas_call | solution.py:585

commit v4 on v3

--- a/solution.py
+++ b/solution.py
@@ -62,6 +62,18 @@
 
 def twice(x, axis=1):
     return jnp.concatenate([x, x], axis=axis)
+
+
+def orders(w):
+    return w, jnp.concatenate([w[LAT:], w[:LAT]], axis=0)
+
+
+def ordered(a, b, part):
+    return jnp.concatenate([a, b] if part % 2 == 0 else [b, a], axis=1)
+
+
+def swapped(w):
+    return w, jnp.concatenate([w[:, LAT:], w[:, :LAT]], axis=1)
 
 
 def kernel(
@@ -114,6 +126,7 @@
     up_pre,
     sums_out,
     sums_in,
+    sums_v,
     acc,
     first_t,
     second_t,
@@ -361,7 +374,7 @@
         own = jnp.concatenate([own.astype(F32), (own << 16).astype(F32)], axis=0)
         acts[b] = half_silu(h + own * scale_all)
 
-    def add_edges(b):
+    def add_edges(b, cut=group_edges):
         lat = dot(first_t[LAT:, :], block(b), 1, 1)
         c = dot(second_t[...], twice(acts[b], 0))
         spread = lax.rsqrt(jnp.mean(c * c, axis=0, keepdims=True) + norm_eps)
@@ -369,15 +382,18 @@
         ids = row(receivers, b)
         position = b * group_edges + lax.broadcasted_iota(I32, (1, group_edges), 1)
         target = jnp.where(position < live[0] * 128, ids >> 8, groups)
-        masked = jnp.concatenate(
-            [
-                updated
-                * jnp.broadcast_to(jnp.where(target == g, 1.0, 0.0).astype(BF16), updated.shape)
-                for g in range(groups)
-            ],
-            axis=0,
-        )
-        acc[...] += dot(masked, hot_columns(ids & (TILE - 1), TILE), 1, 1)
+        masks = [jnp.where(target == g, 1.0, 0.0).astype(BF16) for g in range(groups)]
+        hot = hot_columns(ids & (TILE - 1), TILE)
+
+        def summed(cols):
+            part = updated[:, cols]
+            masked = [part * jnp.broadcast_to(mask[:, cols], part.shape) for mask in masks]
+            return dot(jnp.concatenate(masked, axis=0), hot[:, cols], 1, 1)
+
+        total = summed(slice(0, cut))
+        if cut < group_edges:
+            total = total + summed(slice(cut, group_edges))
+        acc[...] += total
 
     hidden_layer(0)
 
@@ -394,34 +410,45 @@
 
     lax.fori_loop(0, edge_blocks - ahead, full_step, 0)
     lax.fori_loop(edge_blocks - ahead, edge_blocks - 1, last_step, 0)
-    add_edges(edge_blocks - 1)
-
-    fine_out_w, up_out_w = centered(out_w[1]), centered(out_w[2])
-    near = jnp.concatenate([cext[:BORDER, :], cext[3 * BORDER : EDGE_ROWS, :]], axis=0)
-    near_table = dot(near, node_w[1, LAT:, :]).astype(BF16)
-    up_w = jnp.concatenate([node_w[1, :LAT, :], near_table], axis=0)
-    parts = [slice(g * TILE, (g + 1) * TILE) for g in range(groups)]
-    aggs = [acc[g * LAT : (g + 1) * LAT, :].T.astype(BF16) for g in range(groups)]
-    hs = [
-        dot(jnp.concatenate([fine[p, :], agg], axis=1), node_w[0]) for p, agg in zip(parts, aggs)
-    ]
-    cs = [dot(twice(half_silu(0.5 * h)), fine_out_w) for h in hs]
-    news = [
-        (fine[p, :].astype(F32) + scale_rows(c) * gains[1:2, :]).astype(BF16)
-        for p, c in zip(parts, cs)
-    ]
-    for p, new in zip(parts, news):
-        mid[p, :] = new
-    hs = [
-        dot(jnp.concatenate([new, par_near[p, :]], axis=1), up_w) + up_pre[p, :]
-        for p, new in zip(parts, news)
-    ]
-    cs = [dot(twice(half_silu(0.5 * h)), up_out_w) for h in hs]
-    ups = jnp.concatenate([split(scale_rows(c) * gains[2:3, :], 1) for c in cs], axis=0)
-    sums = dot(par_cols[...], ups)
-    sums = sums[:, :LAT] + sums[:, LAT:]
-    sums_out[0] = sums[: 2 * BORDER].astype(BF16)
-    sums_out[1] = sums[2 * BORDER : EDGE_ROWS].astype(BF16)
+    @pl.when(l >= 0)
+    def _():
+        add_edges(edge_blocks - 1, group_edges // 2)
+
+    @pl.when(r >= 0)
+    def _():
+        fine_w, fine_out_w = orders(node_w[0]), orders(centered(out_w[1]))
+        near = jnp.concatenate([cext[:BORDER, :], cext[3 * BORDER : EDGE_ROWS, :]], axis=0)
+        near_table = dot(near, node_w[1, LAT:, :]).astype(BF16)
+        up_w = orders(jnp.concatenate([node_w[1, :LAT, :], near_table], axis=0))
+        up_out_w = orders(centered(out_w[2]))
+        count = nodes // LAT
+        parts = [slice(j * LAT, (j + 1) * LAT) for j in range(count)]
+        hs = []
+        for j, p in enumerate(parts):
+            first = j // 2 * LAT
+            agg = acc[first : first + LAT, j % 2 * LAT : (j % 2 + 1) * LAT].T.astype(BF16)
+            hs.append(dot(ordered(fine[p, :], agg, j), fine_w[j % 2]))
+        cs = [dot(twice(half_silu(0.5 * h)), fine_out_w[j % 2]) for j, h in enumerate(hs)]
+        news = [
+            (fine[p, :].astype(F32) + scale_rows(c) * gains[1:2, :]).astype(BF16)
+            for p, c in zip(parts, cs)
+        ]
+        for p, new in zip(parts, news):
+            mid[p, :] = new
+        hs = [
+            dot(ordered(new, par_near[p, :], j), up_w[j % 2]) + up_pre[p, :]
+            for j, (p, new) in enumerate(zip(parts, news))
+        ]
+        cs = [dot(twice(half_silu(0.5 * h)), up_out_w[j % 2]) for j, h in enumerate(hs)]
+        ups = [split(scale_rows(c) * gains[2:3, :], 1) for c in cs]
+        cut = groups // 2 * 2
+        sums = dot(par_cols[:, : cut * LAT], jnp.concatenate(ups[:cut], axis=0)) + dot(
+            par_cols[:, cut * LAT :], jnp.concatenate(ups[cut:], axis=0)
+        )
+        sums = sums[:, :LAT] + sums[:, LAT:]
+        sums_out[0] = sums[: 2 * BORDER].astype(BF16)
+        sums_out[1] = sums[2 * BORDER : EDGE_ROWS].astype(BF16)
+        sums_v[...] = sums
 
     @pl.when(has_lower)
     def _():
@@ -432,7 +459,7 @@
         sums_up.start()
 
     base = cext[EDGE_ROWS:, :]
-    h = dot(jnp.concatenate([base, sums[EDGE_ROWS:].astype(BF16)], axis=1), node_w[2])
+    h = dot(jnp.concatenate([base, sums_v[EDGE_ROWS:, :].astype(BF16)], axis=1), node_w[2])
     new = scale_rows(dot(twice(half_silu(0.5 * h)), late_out[0])) * gains[3:4, :]
     new = (base.astype(F32) + new).astype(BF16)
     new_inner[...] = new[:inner]
@@ -453,8 +480,8 @@
         sums_up.wait_send()
         sums_down.wait_recv()
 
-    total_edge[: 2 * BORDER, :] = (sums[: 2 * BORDER] + sums_in[0].astype(F32)).astype(BF16)
-    total_edge[2 * BORDER :, :] = (sums[2 * BORDER : EDGE_ROWS] + sums_in[1].astype(F32)).astype(BF16)
+    total_edge[: 2 * BORDER, :] = (sums_v[: 2 * BORDER, :] + sums_in[0].astype(F32)).astype(BF16)
+    total_edge[2 * BORDER :, :] = (sums_v[2 * BORDER : EDGE_ROWS, :] + sums_in[1].astype(F32)).astype(BF16)
 
 
 def finish(
@@ -483,18 +510,21 @@
     coarse_v[BORDER : blocks - BORDER, :] = new_inner[...]
     copies = [pltpu.make_async_copy(coarse_v, coarse_out, sem.at[nodes // TILE])]
     copies[0].start()
-    edge_table = split(dot(new, late_w[1, LAT:, :]), 1)
-    parts = [slice(g * TILE, (g + 1) * TILE) for g in range(nodes // TILE)]
-    found = [dot(par_edge[p, :], edge_table) for p in parts]
+    edge_table = swapped(split(dot(new, late_w[1, LAT:, :]), 1))
+    last_w = orders(late_out[1])
+    parts = [slice(j * LAT, (j + 1) * LAT) for j in range(nodes // LAT)]
+    found = [dot(par_edge[p, :], edge_table[j % 2]) for j, p in enumerate(parts)]
     hs = [down_pre[p, :] + (f[:, :LAT] + f[:, LAT:]) for p, f in zip(parts, found)]
-    cs = [dot(twice(half_silu(0.5 * h)), late_out[1]) for h in hs]
-    for g, c in enumerate(cs):
-        p = parts[g]
+    cs = [dot(twice(half_silu(0.5 * h)), last_w[j % 2]) for j, h in enumerate(hs)]
+    for j, c in enumerate(cs):
+        p = parts[j]
         new = scale_rows(c) * late_gain[4:5, :]
         fine_v[p, :] = (mid[p, :].astype(F32) + new).astype(BF16)
-        part = pl.ds(g * TILE, TILE)
-        copies.append(pltpu.make_async_copy(fine_v.at[part], fine_out.at[part], sem.at[g]))
-        copies[-1].start()
+        if j % 2:
+            g = j // 2
+            part = pl.ds(g * TILE, TILE)
+            copies.append(pltpu.make_async_copy(fine_v.at[part], fine_out.at[part], sem.at[g]))
+            copies[-1].start()
     for copy in copies:
         copy.wait()
 
@@ -568,6 +598,7 @@
             pltpu.VMEM((nodes, LAT), F32),
             pltpu.VMEM((2, 2 * BORDER, LAT), BF16),
             pltpu.VMEM((2, 2 * BORDER, LAT), BF16),
+            pltpu.VMEM((2 * TILE, LAT), F32),
             pltpu.VMEM((groups * LAT, TILE), F32),
             pltpu.VMEM((2 * LAT, LAT), BF16),
             pltpu.VMEM((LAT, 2 * LAT), BF16),

time: 31.5 us -> 31 us (0.984)
  Pallas kernels: 30.1 us -> 29.6 us
    pallas_call x1, Pallas kernels: 28.2 us -> 27.8 us  [body(): pl.pallas_call(functools.partial(kernel, levels), out_shape=(pltpu.VMEM((...]
where the time goes in v4:
time: 31 us; the launch traced here: 30.9 us
  Pallas kernels  29.6 us (95%)
  between operations  1.29 us (4%)
    pallas_call x1, Pallas kernels, body(): pl.pallas_call(functools.partial(kernel, levels), out_shape=(pltpu.VMEM((...  27.8 us
    pallas_call x1, Pallas kernels, body(): pl.pallas_call(finish, out_shape=(jax.ShapeDtypeStruct(fine_nodes.shape,...  1.82 us

profile of v4, /device:TPU:128, one launch (start us, length us, event | category | flops | bytes accessed | tf_op | source)
XLA Modules:
  0.0 30.9 jit_solution(7733766572783957401)
XLA Ops:
  1.3 27.8 %graph_step.1 = (bf16[1280,128]{1,0:T(8,128)(2,1)S(1)}, f32[1280,128]{1,0:T(8,128)S(1)}, bf16[1280,256]{1,0:T(8,128)(2,1)S(1)}, bf16[256,128]{1,0:T(8,128)(2,1)S...) custom-call(bf16[1280,128]{1,0:T(8,128)(2,1)} %fine_h.1, ...), custom_call_target="tpu_custom_call" | custom-call | tf_op jit(solution)/shard_map/graph_step/pallas_call | solution.py:569
  29.1 1.8 %graph_finish.1 = (bf16[1280,128]{1,0:T(8,128)(2,1)}, bf16[320,128]{1,0:T(8,128)(2,1)}) custom-call(bf16[1280,128]{1,0:T(8,128)(2,1)S(1)} %get-tuple-element.11.mid, f32[1280,128]{1,0:T(8,128)S(1)} %get-tuple-element.12.down_pre, bf16[1280,256]{1,0:T(8,128)(2,1)S(1)} %get-tuple-element.13.par_edge, bf16[256,128]{1,0:T(8,128)(2,1)S(1)} %get-tuple-element.14.base_edge, ...), custom_call_target="tpu_custom_call" | custom-call | tf_op jit(solution)/shard_map/graph_finish/pallas_call | solution.py:616

commit v5 on v4

--- a/solution.py
+++ b/solution.py
@@ -20,7 +20,7 @@
 group_edges = 1024
 sub = group_edges // LAT
 TILE = 256
-ahead = 2
+ahead = 3
 lane_tiles = 4
 top = 16380.0
 
@@ -115,7 +115,7 @@
     full,
     sender_q,
     receiver_q,
-    packed,
+    own_terms,
     acts,
     outgoing,
     arrived,
@@ -127,6 +127,7 @@
     sums_out,
     sums_in,
     sums_v,
+    up_v,
     acc,
     first_t,
     second_t,
@@ -269,7 +270,23 @@
     pack(0, lane_tiles, sender_q)
     pack(LAT, nodes // LAT, receiver_q)
 
+    loads[4].wait()
+    loads[5].wait()
+    loads[7].wait()
+    first_t[:LAT, :] = (edge_w[:LAT, :].astype(F32) * 0.5).T.astype(BF16)
+    scale_all = jnp.concatenate([scale_t[...]] * sub, axis=1)
+    skip = lane_tiles * LAT
+
+    def row(ref, b):
+        return jnp.concatenate([ref[pl.ds(b * sub + j, 1), :] for j in range(sub)], axis=1)
+
+    def block(b):
+        return latents[pl.ds(pl.multiple_of(b * group_edges, group_edges), group_edges), :]
+
     def gather(b):
+        h = dot(first_t[:LAT, :], block(b), 1, 1)
+        h = h + dot(table[:, skip:nodes], hot_columns(row(senders, b) - skip, nodes - skip))
+        totals = []
         for j in range(sub):
 
             def look_up(ids, target, x, count):
@@ -282,11 +299,11 @@
 
             s, t = senders[pl.ds(b * sub + j, 1), :], receivers[pl.ds(b * sub + j, 1), :]
             total = look_up(t, receiver_q, None, nodes // LAT)
-            total = total + look_up(s, sender_q, jnp.zeros((HALF, LAT), I32), lane_tiles)
-            packed[b, :, j * LAT : (j + 1) * LAT] = total
-
-    loads[4].wait()
-    loads[5].wait()
+            totals.append(total + look_up(s, sender_q, jnp.zeros((HALF, LAT), I32), lane_tiles))
+        own = jnp.concatenate(totals, axis=1)
+        own = jnp.concatenate([own.astype(F32), (own << 16).astype(F32)], axis=0)
+        own_terms[b] = h + own * scale_all
+
 
     def gather_step(b, carry):
         gather(b)
@@ -314,9 +331,8 @@
         near = jnp.where(ids < float(BORDER), ids, ids + float(2 * BORDER))
         par_near[rows, :] = jnp.where(near == column, 1.0, 0.0).astype(BF16)
 
-    for k in range(7, 12):
+    for k in range(8, 12):
         loads[k].wait()
-    first_t[:LAT, :] = (edge_w[:LAT, :].astype(F32) * 0.5).T.astype(BF16)
     eye = lax.broadcasted_iota(I32, (LAT, LAT), 0) == lax.broadcasted_iota(I32, (LAT, LAT), 1)
     first_t[LAT:, :] = jnp.where(eye, 1.0, 0.0).astype(BF16)
     wide = out_w[0].astype(F32).T
@@ -357,22 +373,10 @@
         table[:, nodes + j * SLOT : nodes + (j + 1) * SLOT] = arrived[j]
 
     gain_all = jnp.concatenate([gain_t[...]] * sub, axis=1)
-    scale_all = jnp.concatenate([scale_t[...]] * sub, axis=1)
-    skip = lane_tiles * LAT
-    listed = table.shape[1]
-
-    def row(ref, b):
-        return jnp.concatenate([ref[pl.ds(b * sub + j, 1), :] for j in range(sub)], axis=1)
-
-    def block(b):
-        return latents[pl.ds(pl.multiple_of(b * group_edges, group_edges), group_edges), :]
 
     def hidden_layer(b):
-        h = dot(first_t[:LAT, :], block(b), 1, 1)
-        h = h + dot(table[:, skip:], hot_columns(row(senders, b) - skip, listed - skip))
-        own = packed[b]
-        own = jnp.concatenate([own.astype(F32), (own << 16).astype(F32)], axis=0)
-        acts[b] = half_silu(h + own * scale_all)
+        hot = hot_columns(row(senders, b) - nodes, slots * SLOT)
+        acts[b] = half_silu(own_terms[b] + dot(table[:, nodes:], hot))
 
     def add_edges(b, cut=group_edges):
         lat = dot(first_t[LAT:, :], block(b), 1, 1)
@@ -441,13 +445,15 @@
         ]
         cs = [dot(twice(half_silu(0.5 * h)), up_out_w[j % 2]) for j, h in enumerate(hs)]
         ups = [split(scale_rows(c) * gains[2:3, :], 1) for c in cs]
+        for p, up in zip(parts, ups):
+            up_v[p, :] = up
         cut = groups // 2 * 2
-        sums = dot(par_cols[:, : cut * LAT], jnp.concatenate(ups[:cut], axis=0)) + dot(
-            par_cols[:, cut * LAT :], jnp.concatenate(ups[cut:], axis=0)
+        sums = dot(par_cols[:EDGE_ROWS, : cut * LAT], jnp.concatenate(ups[:cut], axis=0)) + dot(
+            par_cols[:EDGE_ROWS, cut * LAT :], jnp.concatenate(ups[cut:], axis=0)
         )
         sums = sums[:, :LAT] + sums[:, LAT:]
         sums_out[0] = sums[: 2 * BORDER].astype(BF16)
-        sums_out[1] = sums[2 * BORDER : EDGE_ROWS].astype(BF16)
+        sums_out[1] = sums[2 * BORDER :].astype(BF16)
         sums_v[...] = sums
 
     @pl.when(has_lower)
@@ -459,7 +465,9 @@
         sums_up.start()
 
     base = cext[EDGE_ROWS:, :]
-    h = dot(jnp.concatenate([base, sums_v[EDGE_ROWS:, :].astype(BF16)], axis=1), node_w[2])
+    sums = dot(par_cols[EDGE_ROWS:, :], up_v[...])
+    sums = (sums[:, :LAT] + sums[:, LAT:]).astype(BF16)
+    h = dot(jnp.concatenate([base, sums], axis=1), node_w[2])
     new = scale_rows(dot(twice(half_silu(0.5 * h)), late_out[0])) * gains[3:4, :]
     new = (base.astype(F32) + new).astype(BF16)
     new_inner[...] = new[:inner]
@@ -587,7 +595,7 @@
             pltpu.VMEM((2 * LAT, nodes), F32),
             pltpu.VMEM((HALF, lane_tiles * LAT), I32),
             pltpu.VMEM((HALF, nodes), I32),
-            pltpu.VMEM((edge_blocks, HALF, group_edges), I32),
+            pltpu.VMEM((edge_blocks, LAT, group_edges), F32),
             pltpu.VMEM((edge_blocks, LAT, group_edges), BF16),
             pltpu.VMEM((slots, LAT, SLOT), BF16),
             pltpu.VMEM((slots, LAT, SLOT), BF16),
@@ -598,7 +606,8 @@
             pltpu.VMEM((nodes, LAT), F32),
             pltpu.VMEM((2, 2 * BORDER, LAT), BF16),
             pltpu.VMEM((2, 2 * BORDER, LAT), BF16),
-            pltpu.VMEM((2 * TILE, LAT), F32),
+            pltpu.VMEM((EDGE_ROWS, LAT), F32),
+            pltpu.VMEM((nodes, 2 * LAT), BF16),
             pltpu.VMEM((groups * LAT, TILE), F32),
             pltpu.VMEM((2 * LAT, LAT), BF16),
             pltpu.VMEM((LAT, 2 * LAT), BF16),

time: 31 us -> 30.4 us (0.981)
  Pallas kernels: 29.6 us -> 29 us
    pallas_call x1, Pallas kernels: 27.8 us -> 27.2 us  [body(): pl.pallas_call(functools.partial(kernel, levels), out_shape=(pltpu.VMEM((...]
where the time goes in v5:
time: 30.4 us; the launch traced here: 30.3 us
  Pallas kernels  29 us (95%)
  between operations  1.29 us (4%)
    pallas_call x1, Pallas kernels, body(): pl.pallas_call(functools.partial(kernel, levels), out_shape=(pltpu.VMEM((...  27.2 us
    pallas_call x1, Pallas kernels, body(): pl.pallas_call(finish, out_shape=(jax.ShapeDtypeStruct(fine_nodes.shape,...  1.82 us

profile of v5, /device:TPU:128, one launch (start us, length us, event | category | flops | bytes accessed | tf_op | source)
XLA Modules:
  0.0 30.3 jit_solution(16530303176454101017)
XLA Ops:
  1.3 27.2 %graph_step.1 = (bf16[1280,128]{1,0:T(8,128)(2,1)S(1)}, f32[1280,128]{1,0:T(8,128)S(1)}, bf16[1280,256]{1,0:T(8,128)(2,1)S(1)}, bf16[256,128]{1,0:T(8,128)(2,1)S...) custom-call(bf16[1280,128]{1,0:T(8,128)(2,1)} %fine_h.1, ...), custom_call_target="tpu_custom_call" | custom-call | tf_op jit(solution)/shard_map/graph_step/pallas_call | solution.py:577
  28.4 1.8 %graph_finish.1 = (bf16[1280,128]{1,0:T(8,128)(2,1)}, bf16[320,128]{1,0:T(8,128)(2,1)}) custom-call(bf16[1280,128]{1,0:T(8,128)(2,1)S(1)} %get-tuple-element.11.mid, f32[1280,128]{1,0:T(8,128)S(1)} %get-tuple-element.12.down_pre, bf16[1280,256]{1,0:T(8,128)(2,1)S(1)} %get-tuple-element.13.par_edge, bf16[256,128]{1,0:T(8,128)(2,1)S(1)} %get-tuple-element.14.base_edge, ...), custom_call_target="tpu_custom_call" | custom-call | tf_op jit(solution)/shard_map/graph_finish/pallas_call | solution.py:625

commit v6 on v5

--- a/solution.py
+++ b/solution.py
@@ -20,8 +20,8 @@
 group_edges = 1024
 sub = group_edges // LAT
 TILE = 256
-ahead = 3
-lane_tiles = 4
+ahead = 5
+lane_tiles = 0
 top = 16380.0
 
 
@@ -299,7 +299,9 @@
 
             s, t = senders[pl.ds(b * sub + j, 1), :], receivers[pl.ds(b * sub + j, 1), :]
             total = look_up(t, receiver_q, None, nodes // LAT)
-            totals.append(total + look_up(s, sender_q, jnp.zeros((HALF, LAT), I32), lane_tiles))
+            if lane_tiles:
+                total = total + look_up(s, sender_q, jnp.zeros((HALF, LAT), I32), lane_tiles)
+            totals.append(total)
         own = jnp.concatenate(totals, axis=1)
         own = jnp.concatenate([own.astype(F32), (own << 16).astype(F32)], axis=0)
         own_terms[b] = h + own * scale_all
@@ -593,7 +595,7 @@
         + [
             pltpu.VMEM((LAT, nodes + slots * SLOT), BF16),
             pltpu.VMEM((2 * LAT, nodes), F32),
-            pltpu.VMEM((HALF, lane_tiles * LAT), I32),
+            pltpu.VMEM((HALF, max(lane_tiles, 1) * LAT), I32),
             pltpu.VMEM((HALF, nodes), I32),
             pltpu.VMEM((edge_blocks, LAT, group_edges), F32),
             pltpu.VMEM((edge_blocks, LAT, group_edges), BF16),

time: 30.4 us -> 30 us (0.987)
  Pallas kernels: 29 us -> 28.6 us
    pallas_call x1, Pallas kernels: 27.2 us -> 26.8 us  [body(): pl.pallas_call(functools.partial(kernel, levels), out_shape=(pltpu.VMEM((...]
where the time goes in v6:
time: 30 us; the launch traced here: 29.9 us
  Pallas kernels  28.6 us (95%)
  between operations  1.29 us (4%)
    pallas_call x1, Pallas kernels, body(): pl.pallas_call(functools.partial(kernel, levels), out_shape=(pltpu.VMEM((...  26.8 us
    pallas_call x1, Pallas kernels, body(): pl.pallas_call(finish, out_shape=(jax.ShapeDtypeStruct(fine_nodes.shape,...  1.82 us

profile of v6, /device:TPU:128, one launch (start us, length us, event | category | flops | bytes accessed | tf_op | source)
XLA Modules:
  0.0 29.9 jit_solution(14792026907343487486)
XLA Ops:
  1.3 26.8 %graph_step.1 = (bf16[1280,128]{1,0:T(8,128)(2,1)S(1)}, f32[1280,128]{1,0:T(8,128)S(1)}, bf16[1280,256]{1,0:T(8,128)(2,1)S(1)}, bf16[256,128]{1,0:T(8,128)(2,1)S...) custom-call(bf16[1280,128]{1,0:T(8,128)(2,1)} %fine_h.1, ...), custom_call_target="tpu_custom_call" | custom-call | tf_op jit(solution)/shard_map/graph_step/pallas_call | solution.py:579
  28.0 1.8 %graph_finish.1 = (bf16[1280,128]{1,0:T(8,128)(2,1)}, bf16[320,128]{1,0:T(8,128)(2,1)}) custom-call(bf16[1280,128]{1,0:T(8,128)(2,1)S(1)} %get-tuple-element.11.mid, f32[1280,128]{1,0:T(8,128)S(1)} %get-tuple-element.12.down_pre, bf16[1280,256]{1,0:T(8,128)(2,1)S(1)} %get-tuple-element.13.par_edge, bf16[256,128]{1,0:T(8,128)(2,1)S(1)} %get-tuple-element.14.base_edge, ...), custom_call_target="tpu_custom_call" | custom-call | tf_op jit(solution)/shard_map/graph_finish/pallas_call | solution.py:627
